TPU v7x, 128 devices: a whole 4x4x4 slice. The times are simulated.
128 devices in a mesh: row: 8 (over x, core), col: 16 (over z, y).
Axes of the slice: x: 4, y: 4, z: 4, core: 2. Of those that a mesh axis runs over, the one named last changes fastest.
Arguments:
- raw_vectors: float32 [4096, 81920], P('col', 'row'), may hold values from -810 to 810
- interval_count: int32 [16], replicated, may hold values from 1 to 256, 2048 in all
- cluster_of: int32 [16, 256], P('col'), may hold values from 0 to 31, never falling along the last dimension, each value on 1 to 32 neighbouring positions
- panel_one: float32 [81920, 256], P(('row', 'col')), may hold values from -0.03125 to 0.03125
- factor_one: float32 [256, 256], replicated, may hold values from -0.3 to 2
- panel_two: float32 [81920, 256], P(('row', 'col')), may hold values from -0.03125 to 0.03125
- factor_two: float32 [256, 256], replicated, may hold values from -0.3 to 2
Outputs:
- eigenvectors: float32 [2048, 81920], P('col', 'row')
Inputs may be any that keep to these rules, and one draw needn't show every extreme that they name: `interval_count`: the counts sum to 2048; one is exactly 256. `cluster_of`: labels never fall along an interval's slots; one label covers at most 32 slots, and one covers exactly 32.
All inputs are finite; a program needn't handle non-finite values.
Results may differ from a plain program's by a relative error of at most 0.0003.
Values sent between devices are 32-bit elements; how exact they have to be, the bound alone decides.
A program may use at most 128 MiB of HBM per device.

v0:
```python
import math

import jax
import jax.numpy as jnp
from jax import lax
from jax.sharding import PartitionSpec as P

N = 81920
NB = 16
KD = 128


highest = lax.Precision.HIGHEST


def block_order(counts, column_count, per_device, capacity):
    positions = jnp.arange(column_count * per_device, dtype=jnp.int32)
    device_of = positions // per_device
    local_index = positions % per_device
    rank_of = (local_index // NB * column_count + device_of) * NB + local_index % NB
    interval_end = jnp.cumsum(counts)
    interval_start = interval_end - counts
    owner_device = jnp.sum((interval_end[None, :] <= rank_of[:, None]).astype(jnp.int32), axis=1)
    owner_hit = jnp.arange(column_count, dtype=jnp.int32)[None, :] == owner_device[:, None]
    owner_start = jnp.sum(jnp.where(owner_hit, interval_start[None, :], 0), axis=1)
    return owner_device * capacity + rank_of - owner_start


def finish_block(gram_full, raw_block, labels, is_alive):
    same_group = (labels[:, None] == labels[None, :]) & is_alive[:, None] & is_alive[None, :]
    alive_float = is_alive.astype(jnp.float32)
    masked = jnp.where(same_group, gram_full, 0.0) + jnp.diag(1.0 - alive_float)
    lower_factor = jnp.linalg.cholesky(masked)
    solved = jax.scipy.linalg.solve_triangular(lower_factor, raw_block, lower=True)
    return solved * math.sqrt(N)


def apply_panel(vectors, projected, reflectors, factor):
    scaled = jnp.dot(projected, factor.T, precision=highest, preferred_element_type=jnp.float32)
    return vectors - jnp.einsum("kr,nr->kn", scaled, reflectors, precision=highest)


def project_sum(partial_terms):
    return lax.psum(partial_terms, "row")


def transform(vectors, reflect_one, factor_one, reflect_two, factor_two):
    for reflectors, factor in ((reflect_two, factor_two), (reflect_one, factor_one)):
        partial_terms = jnp.dot(
            vectors, reflectors, precision=highest, preferred_element_type=jnp.float32
        )
        projected = project_sum(partial_terms)
        vectors = apply_panel(vectors, projected, reflectors, factor)
    return vectors


def regroup(vectors):
    return lax.all_to_all(vectors, "col", split_axis=0, concat_axis=1, tiled=True)


def sectioned_order(orthogonal, interval_count, column_count, capacity):
    spread = lax.all_to_all(orthogonal, "col", split_axis=1, concat_axis=0, tiled=True)
    wanted = block_order(interval_count, column_count, KD, capacity)
    return jnp.take(spread, wanted, axis=0)


def body(raw_vectors, interval_count, cluster_of, panel_one, factor_one, panel_two, factor_two):
    column_count = lax.axis_size("col")
    column_index = lax.axis_index("col")
    capacity = raw_vectors.shape[0]
    own_hit = jnp.arange(column_count, dtype=jnp.int32) == column_index
    own_count = jnp.sum(jnp.where(own_hit, interval_count, 0))
    is_alive = jnp.arange(capacity, dtype=jnp.int32) < own_count
    gram_part = jnp.dot(
        raw_vectors, raw_vectors.T, precision=highest, preferred_element_type=jnp.float32
    )
    gram_full = lax.psum(gram_part, "row")
    orthogonal = finish_block(gram_full, raw_vectors, cluster_of[0], is_alive)
    local_rows = regroup(sectioned_order(orthogonal, interval_count, column_count, capacity))
    full_one, full_two = (
        lax.all_gather(panel_one, "col", axis=0, tiled=True),
        lax.all_gather(panel_two, "col", axis=0, tiled=True),
    )
    return transform(local_rows, full_one, factor_one, full_two, factor_two)


def solution(mesh):
    placed = (
        P("col", "row"),
        P(),
        P("col", None),
        P(("row", "col"), None),
        P(),
        P(("row", "col"), None),
        P(),
    )
    return jax.shard_map(
        body, mesh=mesh, in_specs=placed, out_specs=P("col", "row"), check_vma=False
    )
```

profile of v0, /device:TPU:0, one launch (start us, length us, event | category | flops | bytes accessed | tf_op | source)
XLA Modules:
  0.0 624.0 jit_solution(3389111985791579401)
XLA Ops:
  7.4 12.7 %fusion.50 = f32[256,256]{0,1:T(8,128)} fusion(f32[256,10240]{1,0:T(8,128)} %param.7), kind=kOutput, calls=%fused_computation.117 | convolution fusion | flops 8053063680 | bytes 10747904 | tf_op jit(solution)/shard_map/dot_general | solution.py:74
  23.1 61.2 %all-reduce.5.cloned.1.call-done = f32[256,256]{0,1:T(8,128)} async-done(((f32[256,256]{0,1:T(8,128)}), f32[256,256]{0,1:T(8,128)}) %all-reduce.5.cloned.1.call-update) | async-done | bytes 262160 | tf_op jit(solution)/shard_map/psum | solution.py:77
  86.6 11.7 %cholesky.49 = f32[128,128]{1,0:T(8,128)S(1)} custom-call(f32[128,128]{1,0:T(8,128)S(1)} %cholesky.115), custom_call_target="Cholesky" | custom-call | tf_op jit(solution)/shard_map/jit(cholesky)/cholesky | solution.py:33
  98.4 9.8 %custom-call.15 = f32[1,128,128]{1,2,0:T(8,128)S(1)} custom-call(f32[1,128,128]{2,1,0:T(8,128)S(1)} %get-tuple-element.40), custom_call_target="InvertDiagBlocksLowerTriangular" | custom-call | tf_op jit(solution)/shard_map/jit(cholesky)/cholesky | solution.py:33
  108.8 11.7 %cholesky.103 = f32[128,128]{1,0:T(8,128)S(1)} custom-call(f32[128,128]{1,0:T(8,128)S(1)} %convolution_subtract_fusion.3), custom_call_target="Cholesky" | custom-call | tf_op jit(solution)/shard_map/jit(cholesky)/cholesky | solution.py:33
  122.9 4.4 while.1
  127.3 19.7 %custom-call.16 = f32[2,128,128]{1,2,0:T(8,128)S(1)} custom-call(f32[2,128,128]{2,1,0:T(8,128)S(1)} %get-tuple-element.12), custom_call_target="InvertDiagBlocksLowerTriangular" | custom-call | tf_op jit(solution)/shard_map/jit(_solve_triangular)/triangular_solve | solution.py:34
  147.0 6.8 %fusion.1 = f32[128,10240]{1,0:T(8,128)S(1)} fusion(f32[256,10240]{1,0:T(8,128)} %param.7, f32[2,128,128]{1,2,0:T(8,128)S(1)} %custom-call.16), kind=kOutput, calls=%fused_computation.9 | convolution fusion | flops 2013265920 | bytes 10551296 | tf_op jit(solution)/shard_map/jit(_solve_triangular)/triangular_solve | solution.py:34
  156.1 6.4 %fusion = f32[10240,128]{0,1:T(8,128)} fusion(f32[128,10240]{1,0:T(8,128)S(1)} %fusion.1, f32[256,10240]{1,0:T(8,128)S(1)} %copy-done.1, f32[256,256]{0,1:T(8,128)S(1)} %get-tuple-element.98), kind=kOutput, calls=%fused_computation.6 | convolution fusion | flops 2014576640 | bytes 15794176 | tf_op jit(solution)/shard_map/jit(_solve_triangular)/triangular_solve | solution.py:34
  162.5 5.9 copy.56
  168.4 5.5 copy.61
  173.9 6.3 %fusion.5 = f32[128,16,640]{2,0,1:T(8,128)} fusion(f32[16,640,128]{2,1,0:T(8,128)S(1)} %bitcast.76, f32[2,128,128]{1,2,0:T(8,128)S(1)} %custom-call.16), kind=kOutput, calls=%fused_computation.24 | convolution fusion | flops 2013265920 | bytes 10551296 | tf_op jit(solution)/shard_map/jit(_solve_triangular)/triangular_solve | solution.py:34
  180.1 9.0 %maximum_multiply_fusion = f32[256,16,640]{2,0,1:T(8,128)} fusion(f32[128,16,640]{2,0,1:T(8,128)} %fusion.5, f32[128,16,640]{2,0,1:T(8,128)} %bitcast.75), kind=kLoop, calls=%fused_computation.7 | loop fusion | flops 5242880 | bytes 20971520 | tf_op jit(solution)/shard_map/mul | solution.py:35
  189.1 6.8 %all-to-all-start = ((f32[256,16,640]{2,0,1:T(8,128)}), f32[256,16,640]{2,0,1:T(8,128)}, u32[]{:S(2)}, u32[]{:S(2)}) async-start(f32[256,16,640]{2,0,1:T(8,128)} %maximum_multiply_fusion), calls=%async_computation | async-start | bytes 20971520 | tf_op jit(solution)/shard_map/all_to_all | solution.py:62
  196.3 149.8 %all-to-all-done = f32[256,16,640]{2,0,1:T(8,128)} async-done(((f32[256,16,640]{2,0,1:T(8,128)}), f32[256,16,640]{2,0,1:T(8,128)}, u32[]{:S(2)}, u32[]{:S(2)}) %all-to-all-start) | async-done | bytes 10485792 | tf_op jit(solution)/shard_map/all_to_all | solution.py:62
  346.1 14.1 %gather_fusion = f32[2048,640]{1,0:T(8,128)} fusion(f32[4096,640]{1,0:T(8,128)} %bitcast.13, s32[2048]{0:T(1024)S(1)} %broadcast_clamp_fusion), kind=kCustom, calls=%fused_computation | custom fusion | bytes 10493952 | tf_op jit(solution)/shard_map/jit(_take)/gather | solution.py:64
  363.0 63.6 %all_to_all.32 = f32[16,128,640]{2,1,0:T(8,128)S(1)} all-to-all(f32[16,128,640]{2,1,0:T(8,128)S(1)} %broadcast_select_fusion), channel_id=1, replica_groups=mesh['row'=8,'col'=16] {'col'}, dimensions={0} | all-to-all | bytes 10485760 | tf_op jit(solution)/shard_map/all_to_all | solution.py:58
  426.5 2.9 copy.59
  429.4 9.2 %fusion.51 = f32[128,256]{1,0:T(8,128)} fusion(f32[128,10240]{1,0:T(8,128)} %bitcast.72, f32[10240,256]{1,0:T(8,128)} %all-gather.3.cloned.1.call-done), kind=kOutput, calls=%fused_computation.118 | convolution fusion | flops 4026531840 | bytes 15859712 | tf_op jit(solution)/shard_map/dot_general | solution.py:49
  439.3 66.5 %all-reduce.7.cloned.1.call-done = f32[128,256]{1,0:T(8,128)} async-done(((f32[128,256]{1,0:T(8,128)}), f32[128,256]{1,0:T(8,128)}) %all-reduce.7.cloned.1.call-update) | async-done | bytes 131088 | tf_op jit(solution)/shard_map/psum | solution.py:44
  507.1 18.8 %convolution_subtract_fusion.1 = f32[128,10240]{1,0:T(8,128)} fusion(f32[128,10240]{1,0:T(8,128)} %bitcast.73, f32[128,256]{1,0:T(8,128)S(1)} %fusion.52, f32[10240,256]{1,0:T(8,128)} %all-gather.3.cloned.1.call-done), kind=kOutput, calls=%fused_computation.4 | convolution fusion | flops 4027842560 | bytes 21102592 | tf_op jit(solution)/shard_map/kr,nr->kn/dot_general | solution.py:40
  527.6 9.5 %fusion.53 = f32[128,256]{1,0:T(8,128)} fusion(f32[128,10240]{1,0:T(8,128)} %convolution_subtract_fusion.1, f32[10240,256]{1,0:T(8,128)} %all-gather.5.cloned.1.call-done), kind=kOutput, calls=%fused_computation.120 | convolution fusion | flops 4026531840 | bytes 15859712 | tf_op jit(solution)/shard_map/dot_general | solution.py:49
  537.1 59.6 %all-reduce.9.cloned.1.call-done = f32[128,256]{1,0:T(8,128)} async-done(((f32[128,256]{1,0:T(8,128)}), f32[128,256]{1,0:T(8,128)}) %all-reduce.9.cloned.1.call-update) | async-done | bytes 131088 | tf_op jit(solution)/shard_map/psum | solution.py:44
  598.0 18.4 %convolution_subtract_fusion = f32[128,10240]{1,0:T(8,128)} fusion(f32[128,10240]{1,0:T(8,128)} %convolution_subtract_fusion.1, f32[128,256]{1,0:T(8,128)S(1)} %fusion.54, f32[10240,256]{1,0:T(8,128)} %all-gather.5.cloned.1.call-done), kind=kOutput, calls=%fused_computation.3 | convolution fusion | flops 4027842560 | bytes 21102592 | tf_op jit(solution)/shard_map/kr,nr->kn/dot_general | solution.py:40
  (71 shorter events, 21.5 us)
Async XLA Ops:
  7.4 498.4 %copy-start = (f32[256,256]{1,0:T(8,128)S(1)}, f32[256,256]{1,0:T(8,128)}, u32[]{:S(2)}) copy-start(f32[256,256]{1,0:T(8,128)} %param.13) | copy-start | bytes 786436
  7.4 13.3 %copy-start.6 = (s32[16]{0:T(128)S(1)}, s32[16]{0:T(128)}, u32[]{:S(2)}) copy-start(s32[16]{0:T(128)} %param.8) | copy-start | bytes 196
  7.4 76.9 %copy-start.5 = (s32[1,256]{1,0:T(1,128)S(1)}, s32[1,256]{1,0:T(1,128)}, u32[]{:S(2)}) copy-start(s32[1,256]{1,0:T(1,128)} %param.9) | copy-start | bytes 3076
  7.4 76.9 %all-reduce.5.cloned.1.call-start = ((), (), s32[]{:S(2)}) async-start(), calls=%async_computation.2 | async-start | bytes 524288 | tf_op jit(solution)/shard_map/psum | solution.py:77
  20.1 409.3 %all-gather.3.cloned.1.call-start = ((), (), s32[]{:S(2)}) async-start(), calls=%async_computation.3 | async-start | bytes 11141120 | tf_op jit(solution)/shard_map/all_gather | solution.py:82
  147.0 9.1 %copy-start.1 = (f32[256,10240]{1,0:T(8,128)S(1)}, f32[256,10240]{1,0:T(8,128)}, u32[]{:S(2)}) copy-start(f32[256,10240]{1,0:T(8,128)} %param.7) | copy-start | bytes 31457284
  153.8 2.2 copy-start.2
  168.4 5.5 copy-start.3
  189.1 157.0 %all-to-all-start = ((f32[256,16,640]{2,0,1:T(8,128)}), f32[256,16,640]{2,0,1:T(8,128)}, u32[]{:S(2)}, u32[]{:S(2)}) async-start(f32[256,16,640]{2,0,1:T(8,128)} %maximum_multiply_fusion), calls=%async_computation | async-start | bytes 20971520 | tf_op jit(solution)/shard_map/all_to_all | solution.py:62
  195.9 309.9 %all-reduce.7.cloned.1.call-start = ((), (), s32[]{:S(2)}) async-start(), calls=%async_computation.4 | async-start | bytes 262144 | tf_op jit(solution)/shard_map/psum | solution.py:44
  438.7 89.0 %all-gather.5.cloned.1.call-start = ((), (), s32[]{:S(2)}) async-start(), calls=%async_computation.5 | async-start | bytes 11141120 | tf_op jit(solution)/shard_map/all_gather | solution.py:81
  439.3 157.4 %all-reduce.9.cloned.1.call-start = ((), (), s32[]{:S(2)}) async-start(), calls=%async_computation.6 | async-start | bytes 262144 | tf_op jit(solution)/shard_map/psum | solution.py:44
  525.9 70.8 %copy-start.4 = (f32[256,256]{1,0:T(8,128)S(1)}, f32[256,256]{1,0:T(8,128)}, u32[]{:S(2)}) copy-start(f32[256,256]{1,0:T(8,128)} %param.11) | copy-start | bytes 786436
Sparse Core Ops, SparseCore 0:
  20.2 63.9 all-reduce.4
  438.8 66.9 all-reduce.6
  537.3 59.3 all-reduce.8
Sparse Core Ops, SparseCore 1:
  22.7 83.0 all-gather.2
  441.3 86.3 all-gather.4
where the time goes:
time: 627 us; the launch traced here: 624 us
  waiting for transfers between devices  339 us (54%)
  matrix products  91.2 us (15%)
  other arithmetic  70.2 us (11%)
  blocking collectives  63.6 us (10%)
  local copies, waits for them, and re-layouts  35.4 us (6%)
  between operations  16.6 us (3%)
  starting transfers between devices  7.52 us (1%)
    all_to_all x1, waiting for transfers between devices, sectioned_order(): lax.all_to_all(orthogonal, 'col', split_axis=1, concat_axis=0, tiled=True)  150 us
    psum x2, waiting for transfers between devices, project_sum(): return lax.psum(partial_terms, 'row')  126 us
    all_to_all x1, blocking collectives, regroup(): lax.all_to_all(vectors, 'col', split_axis=0, concat_axis=1, tiled=True)  63.6 us
    psum x1, waiting for transfers between devices, body(): gram_full = lax.psum(gram_part, 'row')  61.2 us
    dot_general x2, matrix products, apply_panel(): jnp.einsum('kr,nr->kn', scaled, reflectors, precision=highest)  37.3 us
    another operation x6, other arithmetic, finish_block(): lower_factor = jnp.linalg.cholesky(masked)  34 us
    another operation x3, other arithmetic, finish_block(): jax.scipy.linalg.solve_triangular(lower_factor, raw_block, lower=True)  19.7 us
    another operation x3, matrix products, finish_block(): jax.scipy.linalg.solve_triangular(lower_factor, raw_block, lower=True)  19.5 us
  transfers between devices with their start and end apart: 6, of which 5 were waited for; matrix products, arithmetic and copies ran while one was open for 23% of the time, Pallas kernels for 0%

commit v1 on v0

v1 whole, which is shorter than its diff:
```python
import functools
import math

import jax
import jax.numpy as jnp
from jax import lax
from jax.experimental import pallas as pl
from jax.experimental.pallas import tpu as pltpu
from jax.sharding import PartitionSpec as P

N = 81920
CAP = 256
CM = 32
MESH = pl.DeviceIdType.MESH
COLORS = ((0, 192, (0, 1, 2)), (192, 192, (1, 2, 0)), (384, 128, (2, 0, 1)))
HALF = 512

def locate(x, y, z, core):
    return (x * 2 + core, z * 4 + y)

def sum_kernel(x_ref, out_ref, acc, core_in, ring_a, ring_b, plane_in,
               core_s, core_r, ra_s, ra_r, rb_s, rb_r, pl_s, pl_r, gp_s, gp_r, ga_s, ga_r, gb_s, gb_r, gc_s, gc_r):
    row, col = lax.axis_index("row"), lax.axis_index("col")
    core = lax.rem(row, 2)
    at = (lax.div(row, 2), lax.rem(col, 4), lax.div(col, 4))
    partner = locate(at[0], at[1], at[2], 1 - core)

    def along(axis, step):
        moved = list(at)
        moved[axis] = lax.rem(at[axis] + step + 4, 4)
        return locate(moved[0], moved[1], moved[2], core)

    def send(src, dst, s, r, device):
        copy = pltpu.make_async_remote_copy(src, dst, s, r, device_id=device, device_id_type=MESH)
        copy.start()
        return copy

    mine = core * HALF
    other = (1 - core) * HALF
    copies = [send(x_ref.at[pl.ds(other + p * 128, 128)], core_in.at[pl.ds(p * 128, 128)], core_s.at[p], core_r.at[p], partner) for p in range(4)]
    for p in range(4):
        copies[p].wait()
        acc[p * 128:(p + 1) * 128] = x_ref[pl.ds(mine + p * 128, 128)] + core_in[p * 128:(p + 1) * 128]

    def block(color, step):
        base, tiles, order = COLORS[color]
        return base + lax.rem(at[order[0]] + step + 4, 4) * (tiles // 4)

    copies = []
    for color, (base, tiles, order) in enumerate(COLORS):
        size = tiles // 4
        half = size // 2
        far = block(color, 2)
        slot = base // 4
        copies.append(send(acc.at[pl.ds(far, half)], ring_a.at[pl.ds(slot, half)], ra_s.at[color, 0], ra_r.at[color, 0], along(order[0], 1)))
        copies.append(send(acc.at[pl.ds(far + half, half)], ring_a.at[pl.ds(slot + half, half)], ra_s.at[color, 1], ra_r.at[color, 1], along(order[0], -1)))
    for copy in copies:
        copy.wait()
    for color, (base, tiles, order) in enumerate(COLORS):
        size = tiles // 4
        half = size // 2
        slot = base // 4
        after, before = block(color, 1), block(color, -1)
        acc[pl.ds(after, half)] += ring_a[slot:slot + half]
        acc[pl.ds(before + half, half)] += ring_a[slot + half:slot + size]
    copies = []
    for color, (base, tiles, order) in enumerate(COLORS):
        size = tiles // 4
        slot = base // 4
        copies.append(send(acc.at[pl.ds(block(color, 1), size)], ring_b.at[0, pl.ds(slot, size)], rb_s.at[color, 0], rb_r.at[color, 0], along(order[0], 1)))
        copies.append(send(acc.at[pl.ds(block(color, -1), size)], ring_b.at[1, pl.ds(slot, size)], rb_s.at[color, 1], rb_r.at[color, 1], along(order[0], -1)))
    for copy in copies:
        copy.wait()
    for color, (base, tiles, order) in enumerate(COLORS):
        size = tiles // 4
        slot = base // 4
        acc[pl.ds(block(color, 0), size)] += ring_b[0, slot:slot + size] + ring_b[1, slot:slot + size]

    def peer(color, k):
        order = COLORS[color][2]
        moved = list(at)
        moved[order[1]] = lax.rem(at[order[1]] + k % 4, 4)
        moved[order[2]] = lax.rem(at[order[2]] + k // 4, 4)
        return moved[order[2]] * 4 + moved[order[1]], locate(moved[0], moved[1], moved[2], core)

    copies = []
    for k in range(1, 16):
        for color, (base, tiles, order) in enumerate(COLORS):
            piece = tiles // 64
            slot = base // 64
            which, device = peer(color, k)
            copies.append(send(acc.at[pl.ds(block(color, 0) + which * piece, piece)], plane_in.at[k, pl.ds(slot, piece)], pl_s.at[color, k], pl_r.at[color, k], device))
    for copy in copies:
        copy.wait()
    for color, (base, tiles, order) in enumerate(COLORS):
        piece = tiles // 64
        slot = base // 64
        which, _ = peer(color, 0)
        place = block(color, 0) + which * piece
        total = acc[pl.ds(place, piece)]
        for k in range(1, 16):
            total = total + plane_in[k, slot:slot + piece]
        out_ref[pl.ds(mine + place, piece)] = total
    copies = []
    for k in range(1, 16):
        for color, (base, tiles, order) in enumerate(COLORS):
            piece = tiles // 64
            which, _ = peer(color, 0)
            _, device = peer(color, k)
            spot = out_ref.at[pl.ds(mine + block(color, 0) + which * piece, piece)]
            copies.append(send(spot, spot, gp_s.at[color, k], gp_r.at[color, k], device))
    for copy in copies:
        copy.wait()
    copies = []
    for color, (base, tiles, order) in enumerate(COLORS):
        size = tiles // 4
        spot = out_ref.at[pl.ds(mine + block(color, 0), size)]
        copies.append(send(spot, spot, ga_s.at[color, 0], ga_r.at[color, 0], along(order[0], 1)))
        copies.append(send(spot, spot, ga_s.at[color, 1], ga_r.at[color, 1], along(order[0], -1)))
    for copy in copies:
        copy.wait()
    copies = []
    for color, (base, tiles, order) in enumerate(COLORS):
        size = tiles // 4
        half = size // 2
        first = out_ref.at[pl.ds(mine + block(color, -1), half)]
        second = out_ref.at[pl.ds(mine + block(color, 1) + half, half)]
        copies.append(send(first, first, gb_s.at[color, 0], gb_r.at[color, 0], along(order[0], 1)))
        copies.append(send(second, second, gb_s.at[color, 1], gb_r.at[color, 1], along(order[0], -1)))
    for copy in copies:
        copy.wait()
    spot = out_ref.at[pl.ds(mine, HALF)]
    send(spot, spot, gc_s, gc_r, partner).wait()

def sum_all(tiles):
    D = pltpu.SemaphoreType.DMA
    return pl.pallas_call(sum_kernel, out_shape=jax.ShapeDtypeStruct((1024, 8, 128), jnp.float32),
        in_specs=[pl.BlockSpec(memory_space=pltpu.VMEM)], out_specs=pl.BlockSpec(memory_space=pltpu.VMEM),
        scratch_shapes=[pltpu.VMEM((HALF, 8, 128), jnp.float32), pltpu.VMEM((HALF, 8, 128), jnp.float32),
            pltpu.VMEM((128, 8, 128), jnp.float32), pltpu.VMEM((2, 128, 8, 128), jnp.float32), pltpu.VMEM((16, 8, 8, 128), jnp.float32),
            D((4,)), D((4,)), D((3, 2)), D((3, 2)), D((3, 2)), D((3, 2)), D((3, 16)), D((3, 16)), D((3, 16)), D((3, 16)),
            D((3, 2)), D((3, 2)), D((3, 2)), D((3, 2)), D, D],
        compiler_params=pltpu.CompilerParams(has_side_effects=True))(tiles)


def take_lanes(table, index):
    low, high = table[:, :128], table[:, 128:]
    first, second = index[:, :128], index[:, 128:]
    pick = functools.partial(jnp.take_along_axis, axis=1, mode="promise_in_bounds")
    left = pick(low, first)
    right = jnp.where(second >= 128, pick(high, jnp.maximum(second - 128, 0)), pick(low, jnp.minimum(second, 127)))
    return jnp.concatenate([left, right], axis=1)

def factor_kernel(gram_ref, info_ref, out_ref):
    offset = info_ref[0:1, :]
    alive = info_ref[1:2, :]
    window = gram_ref[...]
    for bit, keep in ((7, 160), (6, 96), (5, 64), (4, 48), (3, 40)):
        shift = 1 << bit
        moved = jnp.concatenate([window[shift:], window[:shift]], axis=0)[:keep]
        window = jnp.where(((offset >> bit) & 1) == 1, moved, window[:keep])
    for bit in (2, 1, 0):
        moved = pltpu.roll(window, 40 - (1 << bit), 0)
        window = jnp.where(((offset >> bit) & 1) == 1, moved, window)
    state = window[:CM]
    lane = lax.broadcasted_iota(jnp.int32, (1, CAP), 1)
    position = lane - offset
    live = alive == 1
    sub = lax.broadcasted_iota(jnp.int32, (CM, CAP), 0)
    for k in range(CM - 1):
        active = (position > k) & live
        index = jnp.broadcast_to(jnp.where(active, offset + k, lane), (CM, CAP))
        pivot_row = take_lanes(state, index)
        pivot = jnp.where(active, pivot_row[k:k + 1], 1.0)
        multiplier = jnp.where(active, state[k:k + 1] / pivot, 0.0)
        updated = jnp.where(sub == k, jnp.where(active, -multiplier, state), state - multiplier * pivot_row)
        state = updated
    spot = jnp.broadcast_to(position, (CM, CAP))
    diagonal = jnp.sum(jnp.where(sub == spot, state, 0.0), axis=0, keepdims=True)
    scale = math.sqrt(N) / jnp.sqrt(jnp.where(live, diagonal, 1.0))
    rows = jnp.where(sub < spot, state, jnp.where(sub == spot, 1.0, 0.0)) * scale
    out_ref[:CM] = jnp.where(live, rows, 0.0)
    out_ref[CM:] = jnp.broadcast_to(offset.astype(jnp.float32), (8, CAP))

def factor_inverse(gram, info):
    return pl.pallas_call(factor_kernel, out_shape=jax.ShapeDtypeStruct((40, CAP), jnp.float32))(gram, info)

def expand_kernel(band_ref, hi_ref, lo_ref):
    offset = band_ref[0, CM:CM + 1, :].astype(jnp.int32)
    wide = jnp.concatenate([band_ref[0, :CM], jnp.zeros((8, CAP), jnp.float32)], axis=0)
    for bit in (0, 1, 2):
        wide = jnp.where(((offset >> bit) & 1) == 1, pltpu.roll(wide, 1 << bit, 0), wide)
    for bit, size in ((3, 48), (4, 64), (5, 96), (6, 160), (7, 256)):
        shift = 1 << bit
        have = wide.shape[0]
        plain = jnp.concatenate([wide, jnp.zeros((size - have, CAP), jnp.float32)], axis=0)
        take = min(have, size - shift)
        parts = [jnp.zeros((shift, CAP), jnp.float32), wide[:take]]
        if size - shift - take:
            parts.append(jnp.zeros((size - shift - take, CAP), jnp.float32))
        wide = jnp.where(((offset >> bit) & 1) == 1, jnp.concatenate(parts, axis=0), plain)
    dense = wide.T
    hi = dense.astype(jnp.bfloat16)
    hi_ref[0] = hi
    lo_ref[0] = (dense - hi.astype(jnp.float32)).astype(jnp.bfloat16)

def expand(bands):
    n = bands.shape[0]
    out = jax.ShapeDtypeStruct((n, CAP, CAP), jnp.bfloat16)
    spec = pl.BlockSpec((1, CAP, CAP), lambda s: (s, 0, 0))
    return pl.pallas_call(expand_kernel, grid=(n,), in_specs=[pl.BlockSpec((1, 40, CAP), lambda s: (s, 0, 0))],
        out_specs=(spec, spec), out_shape=(out, out))(bands)

PREC = lax.Precision.HIGHEST


def split(value):
    hi = value.astype(jnp.bfloat16)
    return hi, (value - hi.astype(jnp.float32)).astype(jnp.bfloat16)


def split_outside(value):
    hi = lax.reduce_precision(value, 8, 7)
    return hi.astype(jnp.bfloat16), (value - hi).astype(jnp.bfloat16)


def dot3(a_hi, a_lo, b_hi, b_lo):
    mul = functools.partial(jnp.dot, preferred_element_type=jnp.float32)
    return mul(a_hi, b_hi) + (mul(a_hi, b_lo) + mul(a_lo, b_hi))


def order_kernel(start_ref, t_hi, t_lo, raw_ref, v_hi, v_lo, ordered_ref, tiles_ref, held):
    step = pl.program_id(0)

    @pl.when(step < 16)
    def _():
        z_hi, z_lo = split(raw_ref[0])
        rows = dot3(t_hi[0], t_lo[0], z_hi, z_lo)
        start = start_ref[jnp.minimum(step, 15)]
        lead = lax.rem(start, 8)
        base = pl.multiple_of(start - lead, 8)
        rows = pltpu.roll(jnp.concatenate([rows, jnp.zeros((8, rows.shape[1]), jnp.float32)], axis=0), lead, 0)
        kept = lax.broadcasted_iota(jnp.int32, (8, rows.shape[1]), 0) < lead
        held[pl.ds(base, 8), :] = jnp.where(kept, held[pl.ds(base, 8), :], rows[:8])
        held[pl.ds(base + 8, CAP), :] = rows[8:]

    @pl.when(step >= 16)
    def _():
        first = pl.multiple_of((step - 16) * 256, 256)
        rows = held[pl.ds(first, 256), :]
        ordered_ref[...] = rows
        r_hi, r_lo = split(rows)
        product = dot3(r_hi, r_lo, v_hi[...], v_lo[...])
        for q in range(4):
            tiles_ref[:, q] = product[:, q * 128:(q + 1) * 128].reshape(32, 8, 128)


def order_rows(starts, t_hi, t_lo, spread, v_hi, v_lo):
    early = lambda s, starts: (jnp.minimum(s, 15), 0, 0)
    late = lambda s: jnp.maximum(s - 16, 0)
    width = spread.shape[2]
    return pl.pallas_call(
        order_kernel,
        grid_spec=pltpu.PrefetchScalarGridSpec(
            num_scalar_prefetch=1,
            grid=(24,),
            in_specs=[
                pl.BlockSpec((1, CAP, CAP), early),
                pl.BlockSpec((1, CAP, CAP), early),
                pl.BlockSpec((1, CAP, width), early),
                pl.BlockSpec((width, 512), lambda s, starts: (0, 0)),
                pl.BlockSpec((width, 512), lambda s, starts: (0, 0)),
            ],
            out_specs=(
                pl.BlockSpec((256, width), lambda s, starts: (late(s), 0)),
                pl.BlockSpec((32, 4, 8, 128), lambda s, starts: (late(s), 0, 0, 0)),
            ),
            scratch_shapes=[pltpu.VMEM((2048 + CAP + 8, width), jnp.float32)],
        ),
        out_shape=(
            jax.ShapeDtypeStruct((2048, width), jnp.float32),
            jax.ShapeDtypeStruct((256, 4, 8, 128), jnp.float32),
        ),
    )(starts, t_hi, t_lo, spread, v_hi, v_lo)


def correct_kernel(ordered_ref, tiles_ref, b_hi, b_lo, out_ref):
    parts = [tiles_ref[:, q].reshape(256, 128) for q in range(4)]
    x_hi, x_lo = split(jnp.concatenate(parts, axis=1))
    result = ordered_ref[...] - dot3(x_hi, x_lo, b_hi[...], b_lo[...])
    out_ref[...] = result.reshape(out_ref.shape)


def correct_rows(ordered, tiles, b_hi, b_lo):
    width = ordered.shape[1]
    return pl.pallas_call(
        correct_kernel,
        grid=(8,),
        in_specs=[
            pl.BlockSpec((256, width), lambda k: (k, 0)),
            pl.BlockSpec((32, 4, 8, 128), lambda k: (k, 0, 0, 0)),
            pl.BlockSpec((512, width), lambda k: (0, 0)),
            pl.BlockSpec((512, width), lambda k: (0, 0)),
        ],
        out_specs=pl.BlockSpec((16, 16, width), lambda k: (0, k, 0)),
        out_shape=jax.ShapeDtypeStruct((16, 128, width), jnp.float32),
    )(ordered, tiles, b_hi, b_lo)


def body(raw_vectors, interval_count, cluster_of, panel_one, factor_one, panel_two, factor_two):
    own = lax.axis_index("col")
    spread = lax.all_to_all(raw_vectors, "col", split_axis=1, concat_axis=0, tiled=True)
    width = spread.shape[1]
    gram = lax.psum(
        jnp.dot(raw_vectors, raw_vectors.T, precision=lax.Precision.HIGH, preferred_element_type=jnp.float32), "row"
    )
    starts = jnp.cumsum(interval_count) - interval_count
    own_count = jnp.sum(jnp.where(jnp.arange(16, dtype=jnp.int32) == own, interval_count, 0))
    slots = jnp.arange(CAP, dtype=jnp.int32)
    labels = cluster_of[0]
    offsets = jnp.sum((labels[None, :] < labels[:, None]).astype(jnp.int32), axis=1)
    info = jnp.stack([offsets, (slots < own_count).astype(jnp.int32)])
    bands = lax.all_gather(factor_inverse(gram, info), "col", axis=0)
    t_hi, t_lo = expand(bands)
    both = jnp.concatenate([panel_two, panel_one], axis=1)
    cross = lax.psum(jnp.dot(panel_two.T, panel_one, precision=PREC), ("row", "col"))
    mul = functools.partial(jnp.dot, precision=PREC)
    one = mul(factor_one.T, panel_one.T)
    two = mul(factor_two.T, panel_two.T - mul(cross, one))
    b_hi, b_lo = split_outside(jnp.concatenate([two, one], axis=0))
    v_hi, v_lo = split_outside(both)
    ordered, tiles = order_rows(starts, t_hi, t_lo, spread.reshape(16, CAP, width), v_hi, v_lo)
    tiles = sum_all(tiles.reshape(1024, 8, 128)).reshape(256, 4, 8, 128)
    blocks = correct_rows(ordered, tiles, b_hi, b_lo)
    return lax.all_to_all(blocks.reshape(2048, width), "col", split_axis=0, concat_axis=1, tiled=True)


def solution(mesh):
    placed = (
        P("col", "row"),
        P(),
        P("col", None),
        P(("row", "col"), None),
        P(),
        P(("row", "col"), None),
        P(),
    )
    return jax.shard_map(
        body, mesh=mesh, in_specs=placed, out_specs=P("col", "row"), check_vma=False
    )
```

time: 627 us -> 576 us (0.919)
  Pallas kernels: 0 us -> 106 us
  matrix products: 91.2 us -> 18.2 us
  other arithmetic: 70.2 us -> 5.29 us
  waiting for transfers between devices: 339 us -> 291 us
  blocking collectives: 63.6 us -> 94.9 us
    all_to_all x1, waiting for transfers between devices: 150 us -> 0.01 us  [body(): lax.all_to_all(raw_vectors, 'col', split_axis=1, concat_axis=0, tiled=True)]
    pallas_call x0 -> x5, Pallas kernels: none -> 106 us  [the longest x1 55.6 us: sum_all(): pl.pallas_call(sum_kernel, out_shape=jax.ShapeDtypeStruct((1024, 8, 128),...]
    psum x3 -> x2, waiting for transfers between devices: 187 us -> 291 us  [the longest x1 235 us: body(): lax.psum(jnp.dot(panel_two.T, panel_one, precision=PREC), ('row', 'col'))]
    another operation x11 -> x3, other arithmetic: 53.9 us -> 0.77 us  [the longest x1 0.61 us: body(): info = jnp.stack([offsets, (slots < own_count).astype(jnp.int32)])]
    dot_general x7 -> x5, matrix products: 71.3 us -> 18.2 us  [the longest x1 12.2 us: body(): jnp.dot(raw_vectors, raw_vectors.T, precision=lax.Precision.HIGH, preferr...]
    all_gather x0 -> x1, blocking collectives: none -> 27 us  [body(): bands = lax.all_gather(factor_inverse(gram, info), 'col', axis=0)]
    all_to_all x1 -> x3, local copies, waits for them, and re-layouts: 2.88 us -> 23 us  [the longest x2 11.8 us: body(): lax.all_to_all(blocks.reshape(2048, width), 'col', split_axis=0, concat_a...]
    another operation x5 -> x0, matrix products: 20 us -> none  [the longest x3 19.5 us: finish_block(): jax.scipy.linalg.solve_triangular(lower_factor, raw_block, lower=True)]
  transfers between devices with their start and end apart: 6 -> 3, of which waited for: 5 -> 2; matrix products, arithmetic and copies ran while one was open for 23% -> 4% of each run, Pallas kernels for 0% -> 3%
where the time goes in v1:
time: 576 us; the launch traced here: 573 us
  waiting for transfers between devices  291 us (51%)
  Pallas kernels  106 us (18%)
  blocking collectives  94.9 us (16%)
  local copies, waits for them, and re-layouts  35 us (6%)
  matrix products  18.2 us (3%)
  between operations  13.6 us (2%)
  starting transfers between devices  8.6 us (1%)
    psum x1, waiting for transfers between devices, body(): lax.psum(jnp.dot(panel_two.T, panel_one, precision=PREC), ('row', 'col'))  235 us
    all_to_all x1, blocking collectives, body(): lax.all_to_all(blocks.reshape(2048, width), 'col', split_axis=0, concat_a...  67.9 us
    psum x1, waiting for transfers between devices, body(): lax.psum(jnp.dot(raw_vectors, raw_vectors.T, precision=lax.Precision.HIGH...  56 us
    pallas_call x1, Pallas kernels, sum_all(): pl.pallas_call(sum_kernel, out_shape=jax.ShapeDtypeStruct((1024, 8, 128),...  55.6 us
    all_gather x1, blocking collectives, body(): bands = lax.all_gather(factor_inverse(gram, info), 'col', axis=0)  27 us
    pallas_call x1, Pallas kernels, order_rows(): pl.pallas_call(order_kernel, grid_spec=pltpu.PrefetchScalarGridSpec(num_s...  25.1 us
    dot_general x1, matrix products, body(): jnp.dot(raw_vectors, raw_vectors.T, precision=lax.Precision.HIGH, preferr...  12.2 us
    all_to_all x2, local copies, waits for them, and re-layouts, body(): lax.all_to_all(blocks.reshape(2048, width), 'col', split_axis=0, concat_a...  11.8 us
  transfers between devices with their start and end apart: 3, of which 2 were waited for; matrix products, arithmetic and copies ran while one was open for 4% of the time, Pallas kernels for 3%

profile of v1, /device:TPU:0, one launch (start us, length us, event | category | flops | bytes accessed | tf_op | source)
XLA Modules:
  0.0 573.1 jit_solution(11560382566409776810)
XLA Ops:
  6.5 11.4 %copy.15 = f32[256,10240]{0,1:T(8,128)} copy(f32[256,10240]{1,0:T(8,128)} %param.7) | data formatting | bytes 20971520 | tf_op args[0]
  18.0 11.2 %copy.16 = f32[256,16,640]{2,0,1:T(8,128)} copy(f32[256,16,640]{0,2,1:T(8,128)} %bitcast.24) | data formatting | bytes 20971520 | tf_op jit(solution)/shard_map/all_to_all | solution.py:312
  29.2 8.3 %all-to-all-start = ((f32[256,16,640]{2,0,1:T(8,128)}), f32[256,16,640]{2,0,1:T(8,128)}, u32[]{:S(2)}, u32[]{:S(2)}) async-start(f32[256,16,640]{2,0,1:T(8,128)} %copy.16), calls=%async_computation | async-start | bytes 20971520 | tf_op jit(solution)/shard_map/all_to_all | solution.py:312
  37.6 1.9 fusion.4
  39.8 12.2 %fusion.3 = f32[256,256]{1,0:T(8,128)} fusion(f32[256,10240]{1,0:T(8,128)} %param.7), kind=kOutput, calls=%fused_computation.16 | convolution fusion | flops 4026531840 | bytes 10747904 | tf_op jit(solution)/shard_map/dot_general | solution.py:315
  52.6 1.1 fusion.2
  53.7 0.6 compare_convert_fusion
  54.4 0.6 pad_add_fusion.info_ref
  55.2 1.4 fusion.5
  56.6 1.3 fusion
  58.0 235.1 %all-reduce.5.cloned.1.call-done = f32[256,256]{1,0:T(8,128)} async-done(((f32[256,256]{1,0:T(8,128)}), f32[256,256]{1,0:T(8,128)}) %all-reduce.5.cloned.1.call-update) | async-done | bytes 262160 | tf_op jit(solution)/shard_map/psum | solution.py:326
  293.1 1.8 convolution_subtract_fusion
  294.9 0.8 convolution_bitcast_fusion
  295.7 1.3 fusion.1
  297.0 56.0 %all-reduce.3.cloned.1.call-done.gram_ref = f32[256,256]{1,0:T(8,128)} async-done(((f32[256,256]{1,0:T(8,128)}), f32[256,256]{1,0:T(8,128)}) %all-reduce.3.cloned.1.call-update) | async-done | bytes 262160 | tf_op jit(solution)/shard_map/psum | solution.py:314
  353.0 4.7 shard_map.73
  357.6 27.0 %all-gather = f32[640,256]{1,0:T(8,128)} all-gather(f32[40,256]{1,0:T(8,128)} %shard_map.73), channel_id=2, replica_groups=mesh['row'=8,'col'=16] {'col'}, dimensions={0}, use_global_device_ids=true | all-gather | bytes 696320 | tf_op jit(solution)/shard_map/all_gather | solution.py:323
  384.7 9.9 %shard_map.74 = (bf16[16,256,256]{2,1,0:T(8,128)(2,1)}, bf16[16,256,256]{2,1,0:T(8,128)(2,1)}) custom-call(f32[16,40,256]{2,1,0:T(8,128)} %bitcast.29), custom_call_target="tpu_custom_call" | custom-call | tf_op jit(solution)/shard_map/pallas_call | solution.py:211
  394.6 25.1 %shard_map.75 = (f32[2048,640]{1,0:T(8,128)}, f32[256,4,8,128]{3,2,1,0:T(8,128)}) custom-call(s32[16]{0:T(128)} %get-tuple-element.18.start_ref, bf16[16,256,256]{2,1,0:T(8,128)(2,1)} %get-tuple-element.9.t_hi, bf16[16,256,256]{2,1,0:T(8,128)(2,1)} %get-tuple-element.10.t_lo, f32[16,256,640]{2,1,0:T(8,128)} %bitcast.5.raw_ref, ...), custom_call_target="tpu_custom_call" | custom-call | tf_op jit(solution)/shard_map/pallas_call | solution.py:262
  419.7 55.6 %shard_map.76 = f32[1024,8,128]{2,1,0:T(8,128)} custom-call(f32[1024,8,128]{2,1,0:T(8,128)} %bitcast.28), custom_call_target="tpu_custom_call" | custom-call | tf_op jit(solution)/shard_map/pallas_call | solution.py:137
  475.3 11.2 %shard_map.77 = f32[16,128,640]{2,1,0:T(8,128)} custom-call(f32[2048,640]{1,0:T(8,128)} %get-tuple-element.11.ordered_ref, f32[256,4,8,128]{3,2,1,0:T(8,128)} %bitcast.27, bf16[512,640]{1,0:T(8,128)(2,1)} %get-tuple-element.14.b_hi, bf16[512,640]{1,0:T(8,128)(2,1)} %get-tuple-element.13.b_lo), custom_call_target="tpu_custom_call" | custom-call | tf_op jit(solution)/shard_map/pallas_call | solution.py:296
  486.5 67.9 %all_to_all.32 = f32[16,128,640]{2,1,0:T(8,128)} all-to-all(f32[16,128,640]{2,1,0:T(8,128)} %shard_map.77), channel_id=1, replica_groups=mesh['row'=8,'col'=16] {'col'}, dimensions={0} | all-to-all | bytes 10485760 | tf_op jit(solution)/shard_map/all_to_all | solution.py:335
  554.4 5.9 %copy.18 = f32[128,16,640]{0,2,1:T(8,128)} copy(f32[128,16,640]{2,0,1:T(8,128)} %bitcast.25) | data formatting | bytes 10485760 | tf_op jit(solution)/shard_map/all_to_all | solution.py:335
  560.3 5.9 %copy.19 = f32[128,10240]{1,0:T(8,128)} copy(f32[128,10240]{0,1:T(8,128)} %bitcast.26) | data formatting | bytes 10485760 | tf_op jit(solution)/shard_map/all_to_all | solution.py:335
  (26 shorter events, 1.1 us)
Async XLA Ops:
  6.5 48.7 %copy-start = (f32[256,256]{1,0:T(8,128)S(1)}, f32[256,256]{1,0:T(8,128)}, u32[]{:S(2)}) copy-start(f32[256,256]{1,0:T(8,128)} %param.11) | copy-start | bytes 786436
  29.2 8.4 %copy-start.2 = (f32[640,256]{1,0:T(8,128)S(1)}, f32[640,256]{1,0:T(8,128)}, u32[]{:S(2)}) copy-start(f32[640,256]{1,0:T(8,128)} %param.12) | copy-start | bytes 1966084
  29.2 8.4 %copy-start.3 = (f32[640,256]{1,0:T(8,128)S(1)}, f32[640,256]{1,0:T(8,128)}, u32[]{:S(2)}) copy-start(f32[640,256]{1,0:T(8,128)} %param.10) | copy-start | bytes 1966084
  29.2 365.4 %all-to-all-start = ((f32[256,16,640]{2,0,1:T(8,128)}), f32[256,16,640]{2,0,1:T(8,128)}, u32[]{:S(2)}, u32[]{:S(2)}) async-start(f32[256,16,640]{2,0,1:T(8,128)} %copy.16), calls=%async_computation | async-start | bytes 20971520 | tf_op jit(solution)/shard_map/all_to_all | solution.py:312
  37.5 255.5 %all-reduce.5.cloned.1.call-start = ((), (), s32[]{:S(2)}) async-start(), calls=%async_computation.3 | async-start | bytes 524288 | tf_op jit(solution)/shard_map/psum | solution.py:326
  39.6 12.8 %copy-start.6 = (s32[16]{0:T(128)S(1)}, s32[16]{0:T(128)}, u32[]{:S(2)}) copy-start(s32[16]{0:T(128)} %param.8) | copy-start | bytes 196
  39.6 14.7 %copy-start.5 = (s32[1,256]{1,0:T(1,128)S(1)}, s32[1,256]{1,0:T(1,128)}, u32[]{:S(2)}) copy-start(s32[1,256]{1,0:T(1,128)} %param.9) | copy-start | bytes 3076
  39.6 313.4 %all-reduce.3.cloned.1.call-start = ((), (), s32[]{:S(2)}) async-start(), calls=%async_computation.2 | async-start | bytes 524288 | tf_op jit(solution)/shard_map/psum | solution.py:314
  55.1 239.7 %copy-start.4 = (f32[256,256]{1,0:T(8,128)S(1)}, f32[256,256]{1,0:T(8,128)}, u32[]{:S(2)}) copy-start(f32[256,256]{1,0:T(8,128)} %param.13) | copy-start | bytes 786436
  560.3 5.9 %copy-start.1 = (f32[256,256]{1,0:T(8,128)S(1)}, f32[256,256]{1,0:T(8,128)}, u32[]{:S(2)}) copy-start(f32[256,256]{1,0:T(8,128)} %param.11) | copy-start | bytes 786436
Sparse Core Ops, SparseCore 0:
  43.1 249.9 all-reduce.4
  295.4 57.5 all-reduce.2

commit v2 on v0

v2 whole, which is shorter than its diff:
```python
import functools
import math

import jax
import jax.numpy as jnp
from jax import lax
from jax.experimental import pallas as pl
from jax.experimental.pallas import tpu as pltpu
from jax.sharding import PartitionSpec as P

N = 81920
CAP = 256
CM = 32
TALL = 272
MESH = pl.DeviceIdType.MESH


def split(value):
    hi = value.astype(jnp.bfloat16)
    return hi, (value - hi.astype(jnp.float32)).astype(jnp.bfloat16)


def dot3(a_hi, a_lo, b_hi, b_lo):
    mul = functools.partial(jnp.dot, preferred_element_type=jnp.float32)
    return mul(a_hi, b_hi) + (mul(a_hi, b_lo) + mul(a_lo, b_hi))


CHUNKS = 8


def back_transform_kernel(
    ordered_rows, v_hi, v_lo, b_hi, b_lo, out,
    part, core_in, acc, ring_a, ring_b, plane_in, whole, result,
    core_s, core_r, ra_s, ra_r, rb_s, rb_r, ps_s, ps_r, pg_s, pg_r, ga_s, ga_r, gb_s, gb_r, gc_s, gc_r,
    move_s, move_r, own_sem,
):
    row, col = lax.axis_index("row"), lax.axis_index("col")
    core, x = lax.rem(row, 2), lax.div(row, 2)
    width = ordered_rows.shape[1]
    partner = (x * 2 + 1 - core, col)
    right = (lax.rem(x + 1, 4) * 2 + core, col)
    left = (lax.rem(x + 3, 4) * 2 + core, col)
    mine, other = core * 16, (1 - core) * 16
    here = x * 4
    after, before, far = lax.rem(x + 1, 4) * 4, lax.rem(x + 3, 4) * 4, lax.rem(x + 2, 4) * 4

    remote = functools.partial(pltpu.make_async_remote_copy, device_id_type=MESH)

    barrier = pltpu.get_barrier_semaphore()

    def greet(device):
        pl.semaphore_signal(barrier, 1, device_id=device, device_id_type=MESH)

    for device in (partner, right, left):
        greet(device)

    def greet_column(k, carry):
        greet((row, lax.rem(col + k, 16)))
        return carry

    lax.fori_loop(1, 16, greet_column, 0)
    pl.semaphore_wait(barrier, 18)

    def core_copy(c):
        return remote(part.at[c, pl.ds(other, 16)], core_in.at[c], core_s.at[c], core_r.at[c], device_id=partner)

    def ring_a_copies(c):
        return (
            remote(acc.at[c, pl.ds(far, 2)], ring_a.at[c, pl.ds(0, 2)], ra_s.at[c, 0], ra_r.at[c, 0], device_id=right),
            remote(acc.at[c, pl.ds(far + 2, 2)], ring_a.at[c, pl.ds(2, 2)], ra_s.at[c, 1], ra_r.at[c, 1], device_id=left),
        )

    def ring_b_copies(c):
        return (
            remote(acc.at[c, pl.ds(after, 4)], ring_b.at[c, 0], rb_s.at[c, 0], rb_r.at[c, 0], device_id=right),
            remote(acc.at[c, pl.ds(before, 4)], ring_b.at[c, 1], rb_s.at[c, 1], rb_r.at[c, 1], device_id=left),
        )

    def plane_copy(c, k):
        peer = lax.rem(col + k, 16)
        source = acc.at[c, here + lax.div(peer, 4), lax.rem(peer, 4)]
        return remote(source, plane_in.at[c, k], ps_s.at[c, k], ps_r.at[c, k], device_id=(row, peer))

    def gather_copy(c, k):
        spot = whole.at[c, mine + here + lax.div(col, 4), lax.rem(col, 4)]
        return remote(spot, spot, pg_s.at[c, k], pg_r.at[c, k], device_id=(row, lax.rem(col + k, 16)))

    def spread_copies(c):
        spot = whole.at[c, pl.ds(mine + here, 4)]
        return (
            remote(spot, spot, ga_s.at[c, 0], ga_r.at[c, 0], device_id=right),
            remote(spot, spot, ga_s.at[c, 1], ga_r.at[c, 1], device_id=left),
        )

    def forward_copies(c):
        first, second = whole.at[c, pl.ds(mine + before, 2)], whole.at[c, pl.ds(mine + after + 2, 2)]
        return (
            remote(first, first, gb_s.at[c, 0], gb_r.at[c, 0], device_id=right),
            remote(second, second, gb_s.at[c, 1], gb_r.at[c, 1], device_id=left),
        )

    def share_copy(c):
        spot = whole.at[c, pl.ds(mine, 16)]
        return remote(spot, spot, gc_s.at[c], gc_r.at[c], device_id=partner)

    def window(c, source):
        return out.at[pl.ds(pl.multiple_of(c * 16, 16), 16), pl.ds(pl.multiple_of(source * width, 128), width)]

    def slab(c, target):
        return result.at[c, pl.ds(pl.multiple_of(target * 16, 16), 16)]

    def move_copy(c, k):
        target = lax.rem(col + k, 16)
        return remote(slab(c, target), window(c, col), move_s.at[c, k], move_r.at[c, k], device_id=(row, target))

    def own_copy(c):
        return pltpu.make_async_copy(slab(c, col), window(c, col), own_sem.at[c])

    def start(*copies):
        for copy in copies:
            copy.start()

    def wait(*copies):
        for copy in copies:
            copy.wait()

    def each(first, last, action):
        def step(k, carry):
            action(k)
            return carry
        lax.fori_loop(first, last, step, 0)

    def ordered(c):
        return ordered_rows[pl.ds(pl.multiple_of(c * 256, 256), 256), :]

    def project(c):
        r_hi, r_lo = split(ordered(c))
        product = dot3(r_hi, r_lo, v_hi[...], v_lo[...])
        for q in range(4):
            part[c, :, q] = product[:, q * 128:(q + 1) * 128].reshape(32, 8, 128)
        start(core_copy(c))

    def fold_core(c):
        wait(core_copy(c))
        acc[c] = part[c, pl.ds(mine, 16)] + core_in[c]
        start(*ring_a_copies(c))

    def fold_a(c):
        wait(*ring_a_copies(c))
        acc[c, pl.ds(after, 2)] += ring_a[c, 0:2]
        acc[c, pl.ds(before + 2, 2)] += ring_a[c, 2:4]
        start(*ring_b_copies(c))

    def fold_b(c):
        wait(*ring_b_copies(c))
        acc[c, pl.ds(here, 4)] += ring_b[c, 0] + ring_b[c, 1]
        each(1, 16, lambda k: plane_copy(c, k).start())

    def fold_plane(c):
        each(1, 16, lambda k: plane_copy(c, k).wait())
        total = acc[c, here + lax.div(col, 4), lax.rem(col, 4)]
        for k in range(1, 16):
            total = total + plane_in[c, k]
        whole[c, mine + here + lax.div(col, 4), lax.rem(col, 4)] = total
        each(1, 16, lambda k: gather_copy(c, k).start())

    def gather_plane(c):
        each(1, 16, lambda k: gather_copy(c, k).wait())
        start(*spread_copies(c))

    def forward(c):
        wait(*spread_copies(c))
        start(*forward_copies(c))

    def share(c):
        wait(*forward_copies(c))
        start(share_copy(c))

    def correct(c):
        wait(share_copy(c))
        x_hi, x_lo = split(jnp.concatenate([whole[c, :, q].reshape(256, 128) for q in range(4)], axis=1))
        result[c] = ordered(c) - dot3(x_hi, x_lo, b_hi[...], b_lo[...])
        each(1, 16, lambda k: move_copy(c, k).start())
        own_copy(c).start()

    stages = (
        (1, fold_core), (2, fold_a), (3, fold_b), (5, fold_plane), (7, gather_plane), (8, forward), (9, share),
        (10, correct), (0, project),
    )

    def tick(t, carry):
        for lag, stage in stages:
            c = t - lag

            @pl.when((c >= 0) & (c < CHUNKS))
            def _(stage=stage, c=c):
                stage(c)

        return carry

    lax.fori_loop(0, CHUNKS + 10, tick, 0)

    def finish(c):
        each(1, 16, lambda k: move_copy(c, k).wait())
        own_copy(c).wait()

    each(0, CHUNKS, finish)


def back_transform(ordered, v_hi, v_lo, b_hi, b_lo):
    width = v_hi.shape[0]
    D, V = pltpu.SemaphoreType.DMA, pltpu.VMEM
    pair = [D((CHUNKS, 2)), D((CHUNKS, 2))]
    many = [D((CHUNKS, 16)), D((CHUNKS, 16))]
    one = [D((CHUNKS,)), D((CHUNKS,))]
    tile = lambda *lead: V((*lead, 8, 128), jnp.float32)
    return pl.pallas_call(
        back_transform_kernel,
        out_shape=jax.ShapeDtypeStruct((128, 16 * width), jnp.float32),
        in_specs=[pl.BlockSpec(memory_space=pltpu.VMEM)] * 5,
        out_specs=pl.BlockSpec(memory_space=pl.ANY),
        scratch_shapes=[
            tile(CHUNKS, 32, 4), tile(CHUNKS, 16, 4), tile(CHUNKS, 16, 4), tile(CHUNKS, 4, 4), tile(CHUNKS, 2, 4, 4),
            tile(CHUNKS, 16), tile(CHUNKS, 32, 4), V((CHUNKS, 256, width), jnp.float32),
            *one, *pair, *pair, *many, *many, *pair, *pair, *one, *many, D((CHUNKS,)),
        ],
        compiler_params=pltpu.CompilerParams(collective_id=7, has_side_effects=True, vmem_limit_bytes=60 * 1024 * 1024),
    )(ordered, v_hi, v_lo, b_hi, b_lo)


def take_lanes(table, index):
    low, high = table[:, :128], table[:, 128:]
    first, second = index[:, :128], index[:, 128:]
    pick = functools.partial(jnp.take_along_axis, axis=1, mode="promise_in_bounds")
    left = pick(low, first)
    right = jnp.where(second >= 128, pick(high, jnp.maximum(second - 128, 0)), pick(low, jnp.minimum(second, 127)))
    return jnp.concatenate([left, right], axis=1)

def factor_kernel(gram_ref, info_ref, out_ref):
    offset = info_ref[0:1, :]
    alive = info_ref[1:2, :]
    window = gram_ref[...]
    for bit, keep in ((7, 160), (6, 96), (5, 64), (4, 48), (3, 40)):
        shift = 1 << bit
        moved = jnp.concatenate([window[shift:], window[:shift]], axis=0)[:keep]
        window = jnp.where(((offset >> bit) & 1) == 1, moved, window[:keep])
    for bit in (2, 1, 0):
        moved = pltpu.roll(window, 40 - (1 << bit), 0)
        window = jnp.where(((offset >> bit) & 1) == 1, moved, window)
    state = window[:CM]
    lane = lax.broadcasted_iota(jnp.int32, (1, CAP), 1)
    position = lane - offset
    live = alive == 1
    sub = lax.broadcasted_iota(jnp.int32, (CM, CAP), 0)
    for k in range(CM - 1):
        active = (position > k) & live
        index = jnp.broadcast_to(jnp.where(active, offset + k, lane), (CM, CAP))
        pivot_row = take_lanes(state, index)
        pivot = jnp.where(active, pivot_row[k:k + 1], 1.0)
        multiplier = jnp.where(active, state[k:k + 1] / pivot, 0.0)
        updated = jnp.where(sub == k, jnp.where(active, -multiplier, state), state - multiplier * pivot_row)
        state = updated
    spot = jnp.broadcast_to(position, (CM, CAP))
    diagonal = jnp.sum(jnp.where(sub == spot, state, 0.0), axis=0, keepdims=True)
    scale = math.sqrt(N) / jnp.sqrt(jnp.where(live, diagonal, 1.0))
    rows = jnp.where(sub < spot, state, jnp.where(sub == spot, 1.0, 0.0)) * scale
    out_ref[:CM] = jnp.where(live, rows, 0.0)
    out_ref[CM:] = jnp.broadcast_to(offset.astype(jnp.float32), (8, CAP))

def factor_inverse(gram, info):
    return pl.pallas_call(factor_kernel, out_shape=jax.ShapeDtypeStruct((40, CAP), jnp.float32))(gram, info)

def expand_kernel(start_ref, band_ref, hi_ref, lo_ref):
    lead = lax.rem(start_ref[pl.program_id(0)], 8)
    offset = band_ref[0, CM:CM + 1, :].astype(jnp.int32)
    wide = jnp.concatenate([band_ref[0, :CM], jnp.zeros((8, CAP), jnp.float32)], axis=0)
    for bit in (0, 1, 2):
        wide = jnp.where(((offset >> bit) & 1) == 1, pltpu.roll(wide, 1 << bit, 0), wide)
    for bit, size in ((3, 48), (4, 64), (5, 96), (6, 160), (7, 256)):
        shift = 1 << bit
        have = wide.shape[0]
        plain = jnp.concatenate([wide, jnp.zeros((size - have, CAP), jnp.float32)], axis=0)
        take = min(have, size - shift)
        parts = [jnp.zeros((shift, CAP), jnp.float32), wide[:take]]
        if size - shift - take:
            parts.append(jnp.zeros((size - shift - take, CAP), jnp.float32))
        wide = jnp.where(((offset >> bit) & 1) == 1, jnp.concatenate(parts, axis=0), plain)
    dense = jnp.concatenate([wide.T, jnp.zeros((TALL - CAP, CAP), jnp.float32)], axis=0)
    hi, lo = split(pltpu.roll(dense, lead, 0))
    hi_ref[0] = hi
    lo_ref[0] = lo


def expand(starts, bands):
    out = jax.ShapeDtypeStruct((16, TALL, CAP), jnp.bfloat16)
    spec = pl.BlockSpec((1, TALL, CAP), lambda s, starts: (s, 0, 0))
    return pl.pallas_call(
        expand_kernel,
        grid_spec=pltpu.PrefetchScalarGridSpec(
            num_scalar_prefetch=1,
            grid=(16,),
            in_specs=[pl.BlockSpec((1, 40, CAP), lambda s, starts: (s, 0, 0))],
            out_specs=(spec, spec),
        ),
        out_shape=(out, out),
    )(starts, bands)


def order_kernel(start_ref, t_hi, t_lo, raw_ref, held):
    start = start_ref[pl.program_id(0)]
    lead = lax.rem(start, 8)
    base = pl.multiple_of(start - lead, 8)
    z_hi, z_lo = split(raw_ref[0])
    rows = dot3(t_hi[0], t_lo[0], z_hi, z_lo)
    kept = lax.broadcasted_iota(jnp.int32, (8, rows.shape[1]), 0) < lead
    held[pl.ds(base, 8), :] = jnp.where(kept, held[pl.ds(base, 8), :], rows[:8])
    held[pl.ds(base + 8, CAP), :] = rows[8:CAP + 8]


def order_rows(starts, t_hi, t_lo, spread):
    width = spread.shape[2]
    factor = pl.BlockSpec((1, TALL, CAP), lambda s, starts: (s, 0, 0))
    return pl.pallas_call(
        order_kernel,
        grid_spec=pltpu.PrefetchScalarGridSpec(
            num_scalar_prefetch=1,
            grid=(16,),
            in_specs=[factor, factor, pl.BlockSpec((1, CAP, width), lambda s, starts: (s, 0, 0))],
            out_specs=pl.BlockSpec((2048 + CAP + 8, width), lambda s, starts: (0, 0)),
        ),
        out_shape=jax.ShapeDtypeStruct((2048 + CAP + 8, width), jnp.float32),
    )(starts, t_hi, t_lo, spread)


def sums_kernel(gram, cross, gram_out, cross_out, gram_in, cross_in, cross_mine, cross_all, s1, r1, s2, r2, s3, r3, s4, r4, s5, r5):
    row, col = lax.axis_index("row"), lax.axis_index("col")
    remote = functools.partial(pltpu.make_async_remote_copy, device_id_type=MESH)
    rows = lambda r: pl.ds(pl.multiple_of(r * 32, 32), 32)
    first, second, third = [], [], []
    for k in range(1, 8):
        peer = lax.rem(row + k, 8)
        first.append(remote(gram.at[rows(peer)], gram_in.at[k], s1.at[k], r1.at[k], device_id=(peer, col)))
        first.append(remote(cross.at[rows(peer)], cross_in.at[k], s2.at[k], r2.at[k], device_id=(peer, col)))
    for copy in first:
        copy.start()
    for copy in first:
        copy.wait()
    gram_sum, cross_sum = gram[rows(row)], cross[rows(row)]
    for k in range(1, 8):
        gram_sum = gram_sum + gram_in[k]
        cross_sum = cross_sum + cross_in[k]
    gram_out[rows(row)] = gram_sum
    cross_mine[...] = cross_sum
    for k in range(1, 16):
        peer = lax.rem(col + k, 16)
        second.append(remote(cross_mine, cross_all.at[k], s3.at[k], r3.at[k], device_id=(row, peer)))
    for k in range(1, 8):
        peer = lax.rem(row + k, 8)
        second.append(remote(gram_out.at[rows(row)], gram_out.at[rows(row)], s4.at[k], r4.at[k], device_id=(peer, col)))
    for copy in second:
        copy.start()
    for copy in second:
        copy.wait()
    for k in range(1, 16):
        cross_sum = cross_sum + cross_all[k]
    cross_out[rows(row)] = cross_sum
    for k in range(1, 8):
        peer = lax.rem(row + k, 8)
        third.append(remote(cross_out.at[rows(row)], cross_out.at[rows(row)], s5.at[k], r5.at[k], device_id=(peer, col)))
    for copy in third:
        copy.start()
    for copy in third:
        copy.wait()


def small_sums(gram, cross):
    D, V = pltpu.SemaphoreType.DMA, pltpu.VMEM
    out = jax.ShapeDtypeStruct((CAP, CAP), jnp.float32)
    vmem = pl.BlockSpec(memory_space=pltpu.VMEM)
    return pl.pallas_call(
        sums_kernel,
        out_shape=(out, out),
        in_specs=[vmem, vmem],
        out_specs=(vmem, vmem),
        scratch_shapes=[
            V((8, 32, CAP), jnp.float32), V((8, 32, CAP), jnp.float32), V((32, CAP), jnp.float32), V((16, 32, CAP), jnp.float32),
            D((8,)), D((8,)), D((8,)), D((8,)), D((16,)), D((16,)), D((8,)), D((8,)), D((8,)), D((8,)),
        ],
        compiler_params=pltpu.CompilerParams(has_side_effects=True),
    )(gram, cross)


def gather_kernel(band, out, s, r):
    row, col = lax.axis_index("row"), lax.axis_index("col")
    copies = []
    for k in range(1, 16):
        peer = lax.rem(col + k, 16)
        copies.append(
            pltpu.make_async_remote_copy(band, out.at[col], s.at[k], r.at[k], device_id=(row, peer), device_id_type=MESH)
        )
    for copy in copies:
        copy.start()
    out[col] = band[...]
    for copy in copies:
        copy.wait()


def gather_bands(band):
    D = pltpu.SemaphoreType.DMA
    vmem = pl.BlockSpec(memory_space=pltpu.VMEM)
    return pl.pallas_call(
        gather_kernel,
        out_shape=jax.ShapeDtypeStruct((16, *band.shape), jnp.float32),
        in_specs=[vmem],
        out_specs=vmem,
        scratch_shapes=[D((16,)), D((16,))],
        compiler_params=pltpu.CompilerParams(has_side_effects=True),
    )(band)


def by_target_kernel(raw, out):
    out[0] = raw[...]


def by_target(raw, width):
    rows = raw.shape[0]
    return pl.pallas_call(
        by_target_kernel,
        grid=(16,),
        in_specs=[pl.BlockSpec((rows, width), lambda t: (0, t))],
        out_specs=pl.BlockSpec((1, rows, width), lambda t: (t, 0, 0)),
        out_shape=jax.ShapeDtypeStruct((16, rows, width), jnp.float32),
    )(raw)


def split_outside(value):
    hi = lax.reduce_precision(value, 8, 7)
    return hi.astype(jnp.bfloat16), (value - hi).astype(jnp.bfloat16)


def body(raw_vectors, interval_count, cluster_of, panel_one, factor_one, panel_two, factor_two):
    own = lax.axis_index("col")
    width = raw_vectors.shape[1] // 16
    spread = lax.all_to_all(by_target(raw_vectors, width), "col", split_axis=0, concat_axis=0)
    mul = functools.partial(jnp.dot, precision=lax.Precision.HIGHEST)
    gram_part = jnp.dot(
        raw_vectors, raw_vectors.T, precision=lax.Precision.HIGH, preferred_element_type=jnp.float32
    )
    gram, cross = small_sums(gram_part, mul(panel_two.T, panel_one))
    starts = jnp.cumsum(interval_count) - interval_count
    own_count = jnp.sum(jnp.where(jnp.arange(16, dtype=jnp.int32) == own, interval_count, 0))
    slots = jnp.arange(CAP, dtype=jnp.int32)
    labels = cluster_of[0]
    offsets = jnp.sum((labels[None, :] < labels[:, None]).astype(jnp.int32), axis=1)
    info = jnp.stack([offsets, (slots < own_count).astype(jnp.int32)])
    t_hi, t_lo = expand(starts, gather_bands(factor_inverse(gram, info)))
    one = mul(factor_one.T, panel_one.T)
    two = mul(factor_two.T, panel_two.T - mul(cross, one))
    b_hi, b_lo = split_outside(jnp.concatenate([two, one], axis=0))
    v_hi, v_lo = split_outside(jnp.concatenate([panel_two, panel_one], axis=1))
    ordered = order_rows(starts, t_hi, t_lo, spread)
    return back_transform(ordered, v_hi, v_lo, b_hi, b_lo)


def solution(mesh):
    placed = (
        P("col", "row"),
        P(),
        P("col", None),
        P(("row", "col"), None),
        P(),
        P(("row", "col"), None),
        P(),
    )
    return jax.shard_map(
        body, mesh=mesh, in_specs=placed, out_specs=P("col", "row"), check_vma=False
    )
```

time: 627 us -> 375 us (0.60)
  waiting for transfers between devices: 339 us -> 0.01 us
  Pallas kernels: 0 us -> 335 us
  matrix products: 91.2 us -> 17.3 us
  other arithmetic: 70.2 us -> 5.42 us
  blocking collectives: 63.6 us -> 0 us
  local copies, waits for them, and re-layouts: 35.4 us -> 6.51 us
  between operations: 16.6 us -> 0.15 us
    pallas_call x0 -> x7, Pallas kernels: none -> 335 us  [the longest x1 154 us: small_sums(): pl.pallas_call(sums_kernel, out_shape=(out, out), in_specs=[vmem, vmem],...]
    psum x3 -> x0, waiting for transfers between devices: 187 us -> none  [the longest x2 126 us: project_sum(): return lax.psum(partial_terms, 'row')]
    all_to_all x1, waiting for transfers between devices: 150 us -> 0.01 us  [body(): lax.all_to_all(by_target(raw_vectors, width), 'col', split_axis=0, concat...]
    all_to_all x1 -> x0, blocking collectives: 63.6 us -> none  [regroup(): lax.all_to_all(vectors, 'col', split_axis=0, concat_axis=1, tiled=True)]
    dot_general x7 -> x5, matrix products: 71.3 us -> 17.3 us  [the longest x1 12.2 us: body(): jnp.dot(raw_vectors, raw_vectors.T, precision=lax.Precision.HIGH, preferr...]
    another operation x11 -> x3, other arithmetic: 53.9 us -> 0.75 us  [the longest x1 0.59 us: body(): info = jnp.stack([offsets, (slots < own_count).astype(jnp.int32)])]
    another operation x5 -> x0, matrix products: 20 us -> none  [the longest x3 19.5 us: finish_block(): jax.scipy.linalg.solve_triangular(lower_factor, raw_block, lower=True)]
    another operation x21 -> x1, local copies, waits for them, and re-layouts: 16 us -> 0.08 us  [the longest x3 11.4 us: finish_block(): jax.scipy.linalg.solve_triangular(lower_factor, raw_block, lower=True)]
  transfers between devices with their start and end apart: 6 -> 1, of which waited for: 5 -> 0; matrix products, arithmetic and copies ran while one was open for 23% -> 6% of each run, Pallas kernels for 0% -> 50%
where the time goes in v2:
time: 375 us; the launch traced here: 372 us
  Pallas kernels  335 us (89%)
  matrix products  17.3 us (5%)
  starting transfers between devices  8.34 us (2%)
  local copies, waits for them, and re-layouts  6.51 us (2%)
  other arithmetic  5.42 us (1%)
    pallas_call x1, Pallas kernels, small_sums(): pl.pallas_call(sums_kernel, out_shape=(out, out), in_specs=[vmem, vmem],...  154 us
    pallas_call x1, Pallas kernels, back_transform(): pl.pallas_call(back_transform_kernel, out_shape=jax.ShapeDtypeStruct((128...  117 us
    pallas_call x1, Pallas kernels, order_rows(): pl.pallas_call(order_kernel, grid_spec=pltpu.PrefetchScalarGridSpec(num_s...  17.7 us
    pallas_call x1, Pallas kernels, gather_bands(): pl.pallas_call(gather_kernel, out_shape=jax.ShapeDtypeStruct((16, *band.s...  17.2 us
    pallas_call x1, Pallas kernels, by_target(): pl.pallas_call(by_target_kernel, grid=(16,), in_specs=[pl.BlockSpec((rows...  12.9 us
    dot_general x1, matrix products, body(): jnp.dot(raw_vectors, raw_vectors.T, precision=lax.Precision.HIGH, preferr...  12.2 us
    pallas_call x1, Pallas kernels, expand(): pl.pallas_call(expand_kernel, grid_spec=pltpu.PrefetchScalarGridSpec(num_...  10.9 us
    all_to_all x1, starting transfers between devices, body(): lax.all_to_all(by_target(raw_vectors, width), 'col', split_axis=0, concat...  8.34 us
  transfers between devices with their start and end apart: 1, of which 0 were waited for; matrix products, arithmetic and copies ran while one was open for 6% of the time, Pallas kernels for 50%

profile of v2, /device:TPU:0, one launch (start us, length us, event | category | flops | bytes accessed | tf_op | source)
XLA Modules:
  0.0 372.3 jit_solution(5734344684947579976)
XLA Ops:
  0.0 12.9 %shard_map.77 = f32[16,256,640]{2,1,0:T(8,128)} custom-call(f32[256,10240]{1,0:T(8,128)} %raw.1), custom_call_target="tpu_custom_call" | custom-call | tf_op jit(solution)/shard_map/pallas_call | solution.py:427
  12.9 8.3 %all-to-all-start = ((f32[16,256,640]{2,1,0:T(8,128)}), f32[16,256,640]{2,1,0:T(8,128)}, u32[]{:S(2)}, u32[]{:S(2)}) async-start(f32[16,256,640]{2,1,0:T(8,128)} %shard_map.77), calls=%async_computation | async-start | bytes 20971520 | tf_op jit(solution)/shard_map/all_to_all | solution.py:444
  21.4 0.1 reduce
  21.6 0.2 copy.11
  21.8 0.6 copy-done.2
  22.4 1.9 fusion.4.cross
  24.3 12.2 %fusion.3.gram = f32[256,256]{1,0:T(8,128)} fusion(f32[256,10240]{1,0:T(8,128)} %raw.1), kind=kOutput, calls=%fused_computation.16 | convolution fusion | flops 4026531840 | bytes 10747904 | tf_op jit(solution)/shard_map/dot_general | solution.py:446
  36.6 154.3 %shard_map.73 = (f32[256,256]{1,0:T(8,128)}, f32[256,256]{1,0:T(8,128)}) custom-call(f32[256,256]{1,0:T(8,128)} %fusion.3.gram, f32[256,256]{1,0:T(8,128)} %fusion.4.cross), custom_call_target="tpu_custom_call" | custom-call | tf_op jit(solution)/shard_map/pallas_call | solution.py:380
  190.8 1.2 fusion.2
  192.1 0.6 compare_convert_fusion
  192.7 0.2 convert_reduce_fusion
  192.9 0.6 pad_add_fusion.info_ref
  193.5 4.7 %shard_map.74.band = f32[40,256]{1,0:T(8,128)} custom-call(f32[256,256]{1,0:T(8,128)} %get-tuple-element.9.gram_ref, s32[2,256]{1,0:T(2,128)} %pad_add_fusion.info_ref), custom_call_target="tpu_custom_call" | custom-call | tf_op jit(solution)/shard_map/pallas_call | solution.py:271
  198.1 17.2 %shard_map.75.band_ref = f32[16,40,256]{2,1,0:T(8,128)} custom-call(f32[40,256]{1,0:T(8,128)} %shard_map.74.band), custom_call_target="tpu_custom_call" | custom-call | tf_op jit(solution)/shard_map/pallas_call | solution.py:411
  215.4 10.9 %shard_map.76 = (bf16[16,272,256]{2,1,0:T(8,128)(2,1)}, bf16[16,272,256]{2,1,0:T(8,128)(2,1)}) custom-call(s32[16]{0:T(128)} %get-tuple-element.18.start_ref, f32[16,40,256]{2,1,0:T(8,128)} %shard_map.75.band_ref), custom_call_target="tpu_custom_call" | custom-call | tf_op jit(solution)/shard_map/pallas_call | solution.py:297
  226.4 1.4 fusion.5
  227.9 0.8 convolution_subtract_fusion
  228.7 0.1 copy-done.4
  228.8 0.9 convolution_bitcast_fusion
  229.7 1.3 fusion.1
  231.0 1.3 fusion
  232.3 17.7 %shard_map.78.ordered_rows = f32[2312,640]{1,0:T(8,128)} custom-call(s32[16]{0:T(128)} %get-tuple-element.18.start_ref, bf16[16,272,256]{2,1,0:T(8,128)(2,1)} %get-tuple-element.10.t_hi, bf16[16,272,256]{2,1,0:T(8,128)(2,1)} %get-tuple-element.11.t_lo, f32[16,256,640]{2,1,0:T(8,128)} %all-to-all-done.raw_ref), custom_call_target="tpu_custom_call" | custom-call | tf_op jit(solution)/shard_map/pallas_call | solution.py:323
  250.0 116.9 %shard_map.79 = f32[128,10240]{1,0:T(8,128)} custom-call(f32[2312,640]{1,0:T(8,128)} %shard_map.78.ordered_rows, bf16[640,512]{1,0:T(8,128)(2,1)} %get-tuple-element.16.v_hi, bf16[640,512]{1,0:T(8,128)(2,1)} %get-tuple-element.15.v_lo, bf16[512,640]{1,0:T(8,128)(2,1)} %get-tuple-element.14.b_hi, bf16[512,640]{1,0:T(8,128)(2,1)} %get-tuple-element.13.b_lo), custom_call_target="tpu_custom_call" | custom-call | tf_op jit(solution)/shard_map/pallas_call | solution.py:217
  366.9 5.3 %copy.14 = f32[128,10240]{1,0:T(8,128)} copy(f32[128,10240]{1,0:T(8,128)} %shard_map.79) | data formatting | bytes 10485760
  (17 shorter events, 0.3 us)
Async XLA Ops:
  0.0 226.4 %copy-start = (f32[256,256]{1,0:T(8,128)S(1)}, f32[256,256]{1,0:T(8,128)}, u32[]{:S(2)}) copy-start(f32[256,256]{1,0:T(8,128)} %param.11) | copy-start | bytes 786436
  12.9 8.4 %copy-start.6 = (s32[16]{0:T(128)S(1)}, s32[16]{0:T(128)}, u32[]{:S(2)}) copy-start(s32[16]{0:T(128)} %param.8) | copy-start | bytes 196
  12.9 8.6 %copy-start.1 = (f32[640,256]{1,0:T(8,128)S(1)}, f32[640,256]{1,0:T(8,128)}, u32[]{:S(2)}) copy-start(f32[640,256]{1,0:T(8,128)} %param.12) | copy-start | bytes 1966084
  12.9 219.4 %all-to-all-start = ((f32[16,256,640]{2,1,0:T(8,128)}), f32[16,256,640]{2,1,0:T(8,128)}, u32[]{:S(2)}, u32[]{:S(2)}) async-start(f32[16,256,640]{2,1,0:T(8,128)} %shard_map.77), calls=%async_computation | async-start | bytes 20971520 | tf_op jit(solution)/shard_map/all_to_all | solution.py:444
  21.3 1.1 copy-start.2
  24.3 168.4 %copy-start.5 = (s32[1,256]{1,0:T(1,128)S(1)}, s32[1,256]{1,0:T(1,128)}, u32[]{:S(2)}) copy-start(s32[1,256]{1,0:T(1,128)} %param.9) | copy-start | bytes 3076
  226.3 1.5 copy-start.3
  227.9 1.0 copy-start.4

commit v3 on v2

--- a/solution.py
+++ b/solution.py
@@ -228,18 +228,34 @@
     )(ordered, v_hi, v_lo, b_hi, b_lo)
 
 
-def take_lanes(table, index):
-    low, high = table[:, :128], table[:, 128:]
-    first, second = index[:, :128], index[:, 128:]
-    pick = functools.partial(jnp.take_along_axis, axis=1, mode="promise_in_bounds")
-    left = pick(low, first)
-    right = jnp.where(second >= 128, pick(high, jnp.maximum(second - 128, 0)), pick(low, jnp.minimum(second, 127)))
-    return jnp.concatenate([left, right], axis=1)
-
-def factor_kernel(gram_ref, info_ref, out_ref):
-    offset = info_ref[0:1, :]
-    alive = info_ref[1:2, :]
-    window = gram_ref[...]
+EARLY = 5
+ROWS = CAP // 8
+
+
+def inverse_band(window, offset, live):
+    lane = lax.broadcasted_iota(jnp.int32, (1, CAP), 1)
+    position = lane - offset
+    sub = lax.broadcasted_iota(jnp.int32, (CM, CAP), 0)
+    state = window
+    for k in range(CM - 1):
+        active = (position > k) & live
+        distance = jnp.where(active, position - k, 0)
+        pivot_row = state
+        for bit in range(5):
+            take = jnp.broadcast_to(((distance >> bit) & 1) == 1, (CM, CAP))
+            pivot_row = jnp.where(take, pltpu.roll(pivot_row, 1 << bit, 1), pivot_row)
+        pivot = jnp.where(active, pivot_row[k:k + 1], 1.0)
+        multiplier = jnp.where(active, state[k:k + 1] / pivot, 0.0)
+        state = jnp.where(sub == k, jnp.where(active, -multiplier, state), state - multiplier * pivot_row)
+    spot = jnp.broadcast_to(position, (CM, CAP))
+    diagonal = jnp.sum(jnp.where(sub == spot, state, 0.0), axis=0, keepdims=True)
+    scale = math.sqrt(N) / jnp.sqrt(jnp.where(live, diagonal, 1.0))
+    rows = jnp.where(sub < spot, state, jnp.where(sub == spot, 1.0, 0.0)) * scale
+    return jnp.where(live, rows, 0.0)
+
+
+def cluster_window(gram, offset):
+    window = gram
     for bit, keep in ((7, 160), (6, 96), (5, 64), (4, 48), (3, 40)):
         shift = 1 << bit
         moved = jnp.concatenate([window[shift:], window[:shift]], axis=0)[:keep]
@@ -247,33 +263,11 @@
     for bit in (2, 1, 0):
         moved = pltpu.roll(window, 40 - (1 << bit), 0)
         window = jnp.where(((offset >> bit) & 1) == 1, moved, window)
-    state = window[:CM]
-    lane = lax.broadcasted_iota(jnp.int32, (1, CAP), 1)
-    position = lane - offset
-    live = alive == 1
-    sub = lax.broadcasted_iota(jnp.int32, (CM, CAP), 0)
-    for k in range(CM - 1):
-        active = (position > k) & live
-        index = jnp.broadcast_to(jnp.where(active, offset + k, lane), (CM, CAP))
-        pivot_row = take_lanes(state, index)
-        pivot = jnp.where(active, pivot_row[k:k + 1], 1.0)
-        multiplier = jnp.where(active, state[k:k + 1] / pivot, 0.0)
-        updated = jnp.where(sub == k, jnp.where(active, -multiplier, state), state - multiplier * pivot_row)
-        state = updated
-    spot = jnp.broadcast_to(position, (CM, CAP))
-    diagonal = jnp.sum(jnp.where(sub == spot, state, 0.0), axis=0, keepdims=True)
-    scale = math.sqrt(N) / jnp.sqrt(jnp.where(live, diagonal, 1.0))
-    rows = jnp.where(sub < spot, state, jnp.where(sub == spot, 1.0, 0.0)) * scale
-    out_ref[:CM] = jnp.where(live, rows, 0.0)
-    out_ref[CM:] = jnp.broadcast_to(offset.astype(jnp.float32), (8, CAP))
-
-def factor_inverse(gram, info):
-    return pl.pallas_call(factor_kernel, out_shape=jax.ShapeDtypeStruct((40, CAP), jnp.float32))(gram, info)
-
-def expand_kernel(start_ref, band_ref, hi_ref, lo_ref):
-    lead = lax.rem(start_ref[pl.program_id(0)], 8)
-    offset = band_ref[0, CM:CM + 1, :].astype(jnp.int32)
-    wide = jnp.concatenate([band_ref[0, :CM], jnp.zeros((8, CAP), jnp.float32)], axis=0)
+    return window[:CM]
+
+
+def dense_rows(band, offset, lead):
+    wide = jnp.concatenate([band, jnp.zeros((8, CAP), jnp.float32)], axis=0)
     for bit in (0, 1, 2):
         wide = jnp.where(((offset >> bit) & 1) == 1, pltpu.roll(wide, 1 << bit, 0), wide)
     for bit, size in ((3, 48), (4, 64), (5, 96), (6, 160), (7, 256)):
@@ -286,24 +280,184 @@
             parts.append(jnp.zeros((size - shift - take, CAP), jnp.float32))
         wide = jnp.where(((offset >> bit) & 1) == 1, jnp.concatenate(parts, axis=0), plain)
     dense = jnp.concatenate([wide.T, jnp.zeros((TALL - CAP, CAP), jnp.float32)], axis=0)
-    hi, lo = split(pltpu.roll(dense, lead, 0))
-    hi_ref[0] = hi
-    lo_ref[0] = lo
-
-
-def expand(starts, bands):
-    out = jax.ShapeDtypeStruct((16, TALL, CAP), jnp.bfloat16)
-    spec = pl.BlockSpec((1, TALL, CAP), lambda s, starts: (s, 0, 0))
+    for bit in range(3):
+        dense = jnp.where(((lead >> bit) & 1) == 1, pltpu.roll(dense, 1 << bit, 0), dense)
+    return dense
+
+
+def front_kernel(
+    counts, raw, labels, panel_one, factor_one, panel_two, factor_two,
+    spread, t_hi, t_lo, v_hi, v_lo, b_hi, b_lo,
+    held, gram_high, gram_low, cross, window, window_in, cross_in, cross_mine, cross_all, cross_sum, band, bands,
+    load_sem, own_sem, move_s, move_r, win_s, win_r, cr_s, cr_r, ca_s, ca_r, cg_s, cg_r, bd_s, bd_r,
+):
+    row, col = lax.axis_index("row"), lax.axis_index("col")
+    width = spread.shape[2]
+    remote = functools.partial(pltpu.make_async_remote_copy, device_id_type=MESH)
+    contract = functools.partial(lax.dot_general, preferred_element_type=jnp.float32)
+    barrier = pltpu.get_barrier_semaphore()
+
+    def each(first, last, action):
+        def step(k, carry):
+            action(k)
+            return carry
+        lax.fori_loop(first, last, step, 0)
+
+    def row_peer(k):
+        return (lax.rem(row + k, 8), col)
+
+    def col_peer(k):
+        return (row, lax.rem(col + k, 16))
+
+    def rows_of(j):
+        return pl.ds(pl.multiple_of(j * ROWS, ROWS), ROWS)
+
+    def load(j):
+        return pltpu.make_async_copy(raw.at[rows_of(j)], held.at[rows_of(j)], load_sem.at[j])
+
+    def move(j, k):
+        target = lax.rem(col + k, 16)
+        part = held.at[rows_of(j), pl.ds(pl.multiple_of(target * width, 128), width)]
+        return remote(part, spread.at[col, rows_of(j)], move_s.at[j, k], move_r.at[j, k], device_id=(row, target))
+
+    each(0, 8, lambda j: load(j).start())
+    each(1, 8, lambda k: pl.semaphore_signal(barrier, 1, device_id=row_peer(k), device_id_type=MESH))
+    each(1, 16, lambda k: pl.semaphore_signal(barrier, 1, device_id=col_peer(k), device_id_type=MESH))
+    pl.semaphore_wait(barrier, 22)
+
+    def send_rows(j):
+        load(j).wait()
+        each(1, 16, lambda k: move(j, k).start())
+
+    each(0, EARLY, send_rows)
+    each(EARLY, 8, lambda j: load(j).wait())
+    own = pltpu.make_async_copy(held.at[:, pl.ds(pl.multiple_of(col * width, 128), width)], spread.at[col], own_sem)
+    own.start()
+
+    gram_high[...] = jnp.zeros_like(gram_high)
+    gram_low[...] = jnp.zeros_like(gram_low)
+    rhs_t = (((1,), (1,)), ((), ()))
+
+    def gram_step(s):
+        hi, lo = split(held[:, pl.ds(pl.multiple_of(s * 1024, 1024), 1024)])
+        gram_high[...] += contract(hi, hi, rhs_t)
+        gram_low[...] += contract(hi, lo, rhs_t)
+
+    each(0, raw.shape[1] // 1024, gram_step)
+    lane = lax.broadcasted_iota(jnp.int32, (1, CAP), 1)
+    label = jnp.broadcast_to(labels[...], (8, CAP))
+    lanes = lax.broadcasted_iota(jnp.int32, (8, CAP), 1)
+    offsets = jnp.where((lanes == 0) | (label != pltpu.roll(label, 1, 1)), lanes, 0)
+    for bit in range(5):
+        shift = 1 << bit
+        offsets = jnp.maximum(offsets, jnp.where(lanes >= shift, pltpu.roll(offsets, shift, 1), 0))
+    offset = offsets[:1]
+    own_start, own_count = jnp.int32(0), jnp.int32(0)
+    for t in range(16):
+        own_start = own_start + jnp.where(t < col, counts[t], 0)
+        own_count = own_count + jnp.where(t == col, counts[t], 0)
+    live = lane < own_count
+    low = gram_low[...]
+    window[...] = cluster_window(gram_high[...] + (low + low.T), offset)
+    one_hi, one_lo = split(panel_one[...])
+    two_hi, two_lo = split(panel_two[...])
+    turned_hi, turned_lo = two_hi.T, two_lo.T
+    cross[...] = dot3(turned_hi, turned_lo, one_hi, one_lo)
+    v_hi[:, :CAP], v_hi[:, CAP:] = two_hi, one_hi
+    v_lo[:, :CAP], v_lo[:, CAP:] = two_lo, one_lo
+
+    def window_copy(k):
+        return remote(window, window_in.at[k], win_s.at[k], win_r.at[k], device_id=row_peer(k))
+
+    def cross_copy(k):
+        return remote(cross.at[rows_of(lax.rem(row + k, 8))], cross_in.at[k], cr_s.at[k], cr_r.at[k], device_id=row_peer(k))
+
+    each(1, 8, lambda k: window_copy(k).start())
+    each(1, 8, lambda k: cross_copy(k).start())
+    each(1, 8, lambda k: window_copy(k).wait())
+    each(1, 8, lambda k: cross_copy(k).wait())
+    piece = cross[rows_of(row)]
+    for k in range(1, 8):
+        piece = piece + cross_in[k]
+    cross_mine[...] = piece
+    window_in[0] = window[...]
+    total = window_in[row]
+    for r in range(1, 8):
+        total = total + window_in[lax.rem(row + 8 - r, 8)]
+    band[:CM] = inverse_band(total, offset, live)
+    band[CM:CM + 1] = offset.astype(jnp.float32)
+    band[CM + 1:CM + 2] = jnp.broadcast_to(lax.rem(own_start, 8), (1, CAP)).astype(jnp.float32)
+    band[CM + 2:] = jnp.zeros((6, CAP), jnp.float32)
+
+    def band_copy(k):
+        return remote(band, bands.at[col], bd_s.at[k], bd_r.at[k], device_id=col_peer(k))
+
+    def cross_all_copy(k):
+        return remote(cross_mine, cross_all.at[k], ca_s.at[k], ca_r.at[k], device_id=col_peer(k))
+
+    def cross_share_copy(k):
+        spot = cross_sum.at[rows_of(row)]
+        return remote(spot, spot, cg_s.at[k], cg_r.at[k], device_id=row_peer(k))
+
+    each(1, 16, lambda k: cross_all_copy(k).start())
+    each(1, 16, lambda k: band_copy(k).start())
+    for j in range(EARLY, 8):
+        each(1, 16, lambda k: move(j, k).start())
+    bands[col] = band[...]
+    f_hi, f_lo = split(factor_one[...].T)
+    one = contract(f_hi, one_hi, rhs_t) + (contract(f_hi, one_lo, rhs_t) + contract(f_lo, one_hi, rhs_t))
+    hi, lo = split(one)
+    b_hi[CAP:], b_lo[CAP:] = hi, lo
+    each(1, 16, lambda k: cross_all_copy(k).wait())
+    piece = cross_mine[...]
+    for k in range(1, 16):
+        piece = piece + cross_all[k]
+    cross_sum[rows_of(row)] = piece
+    each(1, 8, lambda k: cross_share_copy(k).start())
+    each(1, 16, lambda k: band_copy(k).wait())
+
+    def widen(s):
+        hi, lo = split(dense_rows(bands[s, :CM], bands[s, CM:CM + 1].astype(jnp.int32), bands[s, CM + 1:CM + 2].astype(jnp.int32)))
+        t_hi[s], t_lo[s] = hi, lo
+
+    each(0, 16, widen)
+    each(1, 8, lambda k: cross_share_copy(k).wait())
+    c_hi, c_lo = split(cross_sum[...])
+    rest_hi, rest_lo = split(panel_two[...].T - dot3(c_hi, c_lo, b_hi[CAP:], b_lo[CAP:]))
+    f_hi, f_lo = split(factor_two[...].T)
+    hi, lo = split(dot3(f_hi, f_lo, rest_hi, rest_lo))
+    b_hi[:CAP], b_lo[:CAP] = hi, lo
+    own.wait()
+
+    def finish(j):
+        each(1, 16, lambda k: move(j, k).wait())
+
+    each(0, 8, finish)
+
+
+def front(counts, raw, labels, panel_one, factor_one, panel_two, factor_two):
+    D, V = pltpu.SemaphoreType.DMA, pltpu.VMEM
+    width = raw.shape[1] // 16
+    vmem = pl.BlockSpec(memory_space=pltpu.VMEM)
+    hbm = pl.BlockSpec(memory_space=pl.ANY)
+    half = lambda *shape: jax.ShapeDtypeStruct(shape, jnp.bfloat16)
+    tile = lambda *shape: V((*shape, CAP), jnp.float32)
     return pl.pallas_call(
-        expand_kernel,
-        grid_spec=pltpu.PrefetchScalarGridSpec(
-            num_scalar_prefetch=1,
-            grid=(16,),
-            in_specs=[pl.BlockSpec((1, 40, CAP), lambda s, starts: (s, 0, 0))],
-            out_specs=(spec, spec),
+        front_kernel,
+        out_shape=(
+            jax.ShapeDtypeStruct((16, CAP, width), jnp.float32),
+            half(16, TALL, CAP), half(16, TALL, CAP), half(width, 512), half(width, 512), half(512, width), half(512, width),
         ),
-        out_shape=(out, out),
-    )(starts, bands)
+        in_specs=[pl.BlockSpec(memory_space=pltpu.SMEM), hbm, vmem, vmem, vmem, vmem, vmem],
+        out_specs=(hbm, vmem, vmem, vmem, vmem, vmem, vmem),
+        scratch_shapes=[
+            V(raw.shape, jnp.float32), tile(CAP), tile(CAP), tile(CAP), tile(CM), tile(8, CM), tile(8, ROWS), tile(ROWS),
+            tile(16, ROWS), tile(CAP), tile(40), tile(16, 40),
+            D((8,)), D, D((8, 16)), D((8, 16)), D((8,)), D((8,)), D((8,)), D((8,)), D((16,)), D((16,)), D((8,)), D((8,)),
+            D((16,)), D((16,)),
+        ],
+        compiler_params=pltpu.CompilerParams(collective_id=3, has_side_effects=True, vmem_limit_bytes=56 * 1024 * 1024),
+    )(counts, raw, labels, panel_one, factor_one, panel_two, factor_two)
 
 
 def order_kernel(start_ref, t_hi, t_lo, raw_ref, held):
@@ -332,132 +486,11 @@
     )(starts, t_hi, t_lo, spread)
 
 
-def sums_kernel(gram, cross, gram_out, cross_out, gram_in, cross_in, cross_mine, cross_all, s1, r1, s2, r2, s3, r3, s4, r4, s5, r5):
-    row, col = lax.axis_index("row"), lax.axis_index("col")
-    remote = functools.partial(pltpu.make_async_remote_copy, device_id_type=MESH)
-    rows = lambda r: pl.ds(pl.multiple_of(r * 32, 32), 32)
-    first, second, third = [], [], []
-    for k in range(1, 8):
-        peer = lax.rem(row + k, 8)
-        first.append(remote(gram.at[rows(peer)], gram_in.at[k], s1.at[k], r1.at[k], device_id=(peer, col)))
-        first.append(remote(cross.at[rows(peer)], cross_in.at[k], s2.at[k], r2.at[k], device_id=(peer, col)))
-    for copy in first:
-        copy.start()
-    for copy in first:
-        copy.wait()
-    gram_sum, cross_sum = gram[rows(row)], cross[rows(row)]
-    for k in range(1, 8):
-        gram_sum = gram_sum + gram_in[k]
-        cross_sum = cross_sum + cross_in[k]
-    gram_out[rows(row)] = gram_sum
-    cross_mine[...] = cross_sum
-    for k in range(1, 16):
-        peer = lax.rem(col + k, 16)
-        second.append(remote(cross_mine, cross_all.at[k], s3.at[k], r3.at[k], device_id=(row, peer)))
-    for k in range(1, 8):
-        peer = lax.rem(row + k, 8)
-        second.append(remote(gram_out.at[rows(row)], gram_out.at[rows(row)], s4.at[k], r4.at[k], device_id=(peer, col)))
-    for copy in second:
-        copy.start()
-    for copy in second:
-        copy.wait()
-    for k in range(1, 16):
-        cross_sum = cross_sum + cross_all[k]
-    cross_out[rows(row)] = cross_sum
-    for k in range(1, 8):
-        peer = lax.rem(row + k, 8)
-        third.append(remote(cross_out.at[rows(row)], cross_out.at[rows(row)], s5.at[k], r5.at[k], device_id=(peer, col)))
-    for copy in third:
-        copy.start()
-    for copy in third:
-        copy.wait()
-
-
-def small_sums(gram, cross):
-    D, V = pltpu.SemaphoreType.DMA, pltpu.VMEM
-    out = jax.ShapeDtypeStruct((CAP, CAP), jnp.float32)
-    vmem = pl.BlockSpec(memory_space=pltpu.VMEM)
-    return pl.pallas_call(
-        sums_kernel,
-        out_shape=(out, out),
-        in_specs=[vmem, vmem],
-        out_specs=(vmem, vmem),
-        scratch_shapes=[
-            V((8, 32, CAP), jnp.float32), V((8, 32, CAP), jnp.float32), V((32, CAP), jnp.float32), V((16, 32, CAP), jnp.float32),
-            D((8,)), D((8,)), D((8,)), D((8,)), D((16,)), D((16,)), D((8,)), D((8,)), D((8,)), D((8,)),
-        ],
-        compiler_params=pltpu.CompilerParams(has_side_effects=True),
-    )(gram, cross)
-
-
-def gather_kernel(band, out, s, r):
-    row, col = lax.axis_index("row"), lax.axis_index("col")
-    copies = []
-    for k in range(1, 16):
-        peer = lax.rem(col + k, 16)
-        copies.append(
-            pltpu.make_async_remote_copy(band, out.at[col], s.at[k], r.at[k], device_id=(row, peer), device_id_type=MESH)
-        )
-    for copy in copies:
-        copy.start()
-    out[col] = band[...]
-    for copy in copies:
-        copy.wait()
-
-
-def gather_bands(band):
-    D = pltpu.SemaphoreType.DMA
-    vmem = pl.BlockSpec(memory_space=pltpu.VMEM)
-    return pl.pallas_call(
-        gather_kernel,
-        out_shape=jax.ShapeDtypeStruct((16, *band.shape), jnp.float32),
-        in_specs=[vmem],
-        out_specs=vmem,
-        scratch_shapes=[D((16,)), D((16,))],
-        compiler_params=pltpu.CompilerParams(has_side_effects=True),
-    )(band)
-
-
-def by_target_kernel(raw, out):
-    out[0] = raw[...]
-
-
-def by_target(raw, width):
-    rows = raw.shape[0]
-    return pl.pallas_call(
-        by_target_kernel,
-        grid=(16,),
-        in_specs=[pl.BlockSpec((rows, width), lambda t: (0, t))],
-        out_specs=pl.BlockSpec((1, rows, width), lambda t: (t, 0, 0)),
-        out_shape=jax.ShapeDtypeStruct((16, rows, width), jnp.float32),
-    )(raw)
-
-
-def split_outside(value):
-    hi = lax.reduce_precision(value, 8, 7)
-    return hi.astype(jnp.bfloat16), (value - hi).astype(jnp.bfloat16)
-
-
 def body(raw_vectors, interval_count, cluster_of, panel_one, factor_one, panel_two, factor_two):
-    own = lax.axis_index("col")
-    width = raw_vectors.shape[1] // 16
-    spread = lax.all_to_all(by_target(raw_vectors, width), "col", split_axis=0, concat_axis=0)
-    mul = functools.partial(jnp.dot, precision=lax.Precision.HIGHEST)
-    gram_part = jnp.dot(
-        raw_vectors, raw_vectors.T, precision=lax.Precision.HIGH, preferred_element_type=jnp.float32
+    spread, t_hi, t_lo, v_hi, v_lo, b_hi, b_lo = front(
+        interval_count, raw_vectors, cluster_of, panel_one, factor_one, panel_two, factor_two
     )
-    gram, cross = small_sums(gram_part, mul(panel_two.T, panel_one))
     starts = jnp.cumsum(interval_count) - interval_count
-    own_count = jnp.sum(jnp.where(jnp.arange(16, dtype=jnp.int32) == own, interval_count, 0))
-    slots = jnp.arange(CAP, dtype=jnp.int32)
-    labels = cluster_of[0]
-    offsets = jnp.sum((labels[None, :] < labels[:, None]).astype(jnp.int32), axis=1)
-    info = jnp.stack([offsets, (slots < own_count).astype(jnp.int32)])
-    t_hi, t_lo = expand(starts, gather_bands(factor_inverse(gram, info)))
-    one = mul(factor_one.T, panel_one.T)
-    two = mul(factor_two.T, panel_two.T - mul(cross, one))
-    b_hi, b_lo = split_outside(jnp.concatenate([two, one], axis=0))
-    v_hi, v_lo = split_outside(jnp.concatenate([panel_two, panel_one], axis=1))
     ordered = order_rows(starts, t_hi, t_lo, spread)
     return back_transform(ordered, v_hi, v_lo, b_hi, b_lo)
 

time: 375 us -> 288 us (0.77)
  Pallas kernels: 335 us -> 280 us
  matrix products: 17.3 us -> 0 us
  starting transfers between devices: 8.34 us -> 0 us
  other arithmetic: 5.42 us -> 1.32 us
    pallas_call x5 -> x1, Pallas kernels: 200 us -> 145 us  [front(): pl.pallas_call(front_kernel, out_shape=(jax.ShapeDtypeStruct((16, CAP, wi...]
    dot_general x5 -> x0, matrix products: 17.3 us -> none  [the longest x1 12.2 us: body(): jnp.dot(raw_vectors, raw_vectors.T, precision=lax.Precision.HIGH, preferr...]
    all_to_all x1 -> x0, starting transfers between devices: 8.34 us -> none  [body(): lax.all_to_all(by_target(raw_vectors, width), 'col', split_axis=0, concat...]
  transfers between devices with their start and end apart: 1 -> 0, of which waited for: 0 -> 0; matrix products, arithmetic and copies ran while one was open for 6% -> 0% of each run, Pallas kernels for 50% -> 0%
where the time goes in v3:
time: 288 us
  Pallas kernels  280 us (97%)
  local copies, waits for them, and re-layouts  6.08 us (2%)
    pallas_call x1, Pallas kernels, front(): pl.pallas_call(front_kernel, out_shape=(jax.ShapeDtypeStruct((16, CAP, wi...  145 us
    pallas_call x1, Pallas kernels, back_transform(): pl.pallas_call(back_transform_kernel, out_shape=jax.ShapeDtypeStruct((128...  118 us
    pallas_call x1, Pallas kernels, order_rows(): pl.pallas_call(order_kernel, grid_spec=pltpu.PrefetchScalarGridSpec(num_s...  17.7 us

profile of v3, /device:TPU:0, one launch (start us, length us, event | category | flops | bytes accessed | tf_op | source)
XLA Modules:
  0.0 287.5 jit_solution(9238000697940696084)
XLA Ops:
  0.0 0.7 copy.9
  0.8 0.1 reduce
  0.9 1.2 sub.3.start_ref
  2.1 144.6 %shard_map.73 = (f32[16,256,640]{2,1,0:T(8,128)}, bf16[16,272,256]{2,1,0:T(8,128)(2,1)}, bf16[16,272,256]{2,1,0:T(8,128)(2,1)}, bf16[640,512]{1,0:T(8,128)(2,1)}...) custom-call(s32[16]{0:T(128)} %counts.1, f32[256,10240]{1,0:T(8,128)} %raw.1, ...), custom_call_target="tpu_custom_call" | custom-call | tf_op jit(solution)/shard_map/pallas_call | solution.py:445
  146.7 17.7 %shard_map.74.ordered_rows = f32[2312,640]{1,0:T(8,128)} custom-call(s32[16]{0:T(128)} %sub.3.start_ref, bf16[16,272,256]{2,1,0:T(8,128)(2,1)} %get-tuple-element.12.t_hi, bf16[16,272,256]{2,1,0:T(8,128)(2,1)} %get-tuple-element.13.t_lo, f32[16,256,640]{2,1,0:T(8,128)} %get-tuple-element.14.raw_ref), custom_call_target="tpu_custom_call" | custom-call | tf_op jit(solution)/shard_map/pallas_call | solution.py:477
  164.4 117.8 %shard_map.75 = f32[128,10240]{1,0:T(8,128)} custom-call(f32[2312,640]{1,0:T(8,128)} %shard_map.74.ordered_rows, bf16[640,512]{1,0:T(8,128)(2,1)} %get-tuple-element.15.v_hi, bf16[640,512]{1,0:T(8,128)(2,1)} %get-tuple-element.16.v_lo, bf16[512,640]{1,0:T(8,128)(2,1)} %get-tuple-element.17.b_hi, bf16[512,640]{1,0:T(8,128)(2,1)} %get-tuple-element.18.b_lo), custom_call_target="tpu_custom_call" | custom-call | tf_op jit(solution)/shard_map/pallas_call | solution.py:217
  282.2 5.3 %copy.11 = f32[128,10240]{1,0:T(8,128)} copy(f32[128,10240]{1,0:T(8,128)} %shard_map.75) | data formatting | bytes 10485760
  (1 shorter events, 0.0 us)

commit v4 on v3

--- a/solution.py
+++ b/solution.py
@@ -29,10 +29,10 @@
 
 
 def back_transform_kernel(
-    ordered_rows, v_hi, v_lo, b_hi, b_lo, out,
-    part, core_in, acc, ring_a, ring_b, plane_in, whole, result,
+    rows_in, v_hi_in, v_lo_in, b_hi_in, b_lo_in, out,
+    ordered_rows, v_hi, v_lo, b_hi, b_lo, part, core_in, acc, ring_a, ring_b, plane_in, whole, result,
     core_s, core_r, ra_s, ra_r, rb_s, rb_r, ps_s, ps_r, pg_s, pg_r, ga_s, ga_r, gb_s, gb_r, gc_s, gc_r,
-    move_s, move_r, own_sem,
+    move_s, move_r, own_sem, rows_sem, panel_sem,
 ):
     row, col = lax.axis_index("row"), lax.axis_index("col")
     core, x = lax.rem(row, 2), lax.div(row, 2)
@@ -46,6 +46,21 @@
 
     remote = functools.partial(pltpu.make_async_remote_copy, device_id_type=MESH)
 
+    panels = [
+        pltpu.make_async_copy(source, target, panel_sem.at[i])
+        for i, (source, target) in enumerate(((v_hi_in, v_hi), (v_lo_in, v_lo), (b_hi_in, b_hi), (b_lo_in, b_lo)))
+    ]
+
+    def load(c):
+        rows = pl.ds(pl.multiple_of(c * 256, 256), 256)
+        return pltpu.make_async_copy(rows_in.at[rows], ordered_rows.at[rows], rows_sem.at[c])
+
+    panels[0].start()
+    panels[1].start()
+    for c in range(CHUNKS):
+        load(c).start()
+    panels[2].start()
+    panels[3].start()
     barrier = pltpu.get_barrier_semaphore()
 
     def greet(device):
@@ -60,6 +75,8 @@
 
     lax.fori_loop(1, 16, greet_column, 0)
     pl.semaphore_wait(barrier, 18)
+    panels[0].wait()
+    panels[1].wait()
 
     def core_copy(c):
         return remote(part.at[c, pl.ds(other, 16)], core_in.at[c], core_s.at[c], core_r.at[c], device_id=partner)
@@ -134,6 +151,7 @@
         return ordered_rows[pl.ds(pl.multiple_of(c * 256, 256), 256), :]
 
     def project(c):
+        load(c).wait()
         r_hi, r_lo = split(ordered(c))
         product = dot3(r_hi, r_lo, v_hi[...], v_lo[...])
         for q in range(4):
@@ -198,7 +216,10 @@
 
         return carry
 
-    lax.fori_loop(0, CHUNKS + 10, tick, 0)
+    lax.fori_loop(0, 8, tick, 0)
+    panels[2].wait()
+    panels[3].wait()
+    lax.fori_loop(8, CHUNKS + 10, tick, 0)
 
     def finish(c):
         each(1, 16, lambda k: move_copy(c, k).wait())
@@ -217,18 +238,19 @@
     return pl.pallas_call(
         back_transform_kernel,
         out_shape=jax.ShapeDtypeStruct((128, 16 * width), jnp.float32),
-        in_specs=[pl.BlockSpec(memory_space=pltpu.VMEM)] * 5,
+        in_specs=[pl.BlockSpec(memory_space=pl.ANY)] * 5,
         out_specs=pl.BlockSpec(memory_space=pl.ANY),
         scratch_shapes=[
+            V((256 * CHUNKS, width), jnp.float32), V((width, 512), jnp.bfloat16), V((width, 512), jnp.bfloat16),
+            V((512, width), jnp.bfloat16), V((512, width), jnp.bfloat16),
             tile(CHUNKS, 32, 4), tile(CHUNKS, 16, 4), tile(CHUNKS, 16, 4), tile(CHUNKS, 4, 4), tile(CHUNKS, 2, 4, 4),
             tile(CHUNKS, 16), tile(CHUNKS, 32, 4), V((CHUNKS, 256, width), jnp.float32),
-            *one, *pair, *pair, *many, *many, *pair, *pair, *one, *many, D((CHUNKS,)),
+            *one, *pair, *pair, *many, *many, *pair, *pair, *one, *many, D((CHUNKS,)), D((CHUNKS,)), D((4,)),
         ],
         compiler_params=pltpu.CompilerParams(collective_id=7, has_side_effects=True, vmem_limit_bytes=60 * 1024 * 1024),
     )(ordered, v_hi, v_lo, b_hi, b_lo)
 
 
-EARLY = 5
 ROWS = CAP // 8
 
 
@@ -288,8 +310,10 @@
 def front_kernel(
     counts, raw, labels, panel_one, factor_one, panel_two, factor_two,
     spread, t_hi, t_lo, v_hi, v_lo, b_hi, b_lo,
-    held, gram_high, gram_low, cross, window, window_in, cross_in, cross_mine, cross_all, cross_sum, band, bands,
-    load_sem, own_sem, move_s, move_r, win_s, win_r, cr_s, cr_r, ca_s, ca_r, cg_s, cg_r, bd_s, bd_r,
+    held, gram_high, gram_low, cross, window, window_in, cross_in, cross_mine, cross_y, cross_z, cross_part, cross_sum,
+    band, bands, wide_hi, wide_lo,
+    load_sem, own_sem, move_s, move_r, win_s, win_r, cr_s, cr_r, cy_s, cy_r, cz_s, cz_r, cp_s, cp_r, cg_s, cg_r,
+    bd_s, bd_r, wide_sem,
 ):
     row, col = lax.axis_index("row"), lax.axis_index("col")
     width = spread.shape[2]
@@ -329,14 +353,60 @@
         load(j).wait()
         each(1, 16, lambda k: move(j, k).start())
 
-    each(0, EARLY, send_rows)
-    each(EARLY, 8, lambda j: load(j).wait())
+    y, z = lax.rem(col, 4), lax.div(col, 4)
+    rhs_t = (((1,), (1,)), ((), ()))
+
+    def y_peer(k):
+        return (row, z * 4 + lax.rem(y + k, 4))
+
+    def z_peer(k):
+        return (row, lax.rem(z + k, 4) * 4 + y)
+
+    def eight(i):
+        return pl.ds(pl.multiple_of(i * 8, 8), 8)
+
+    def cross_copy(k):
+        return remote(cross.at[rows_of(lax.rem(row + k, 8))], cross_in.at[k], cr_s.at[k], cr_r.at[k], device_id=row_peer(k))
+
+    def cross_y_copy(k):
+        return remote(cross_mine.at[eight(lax.rem(y + k, 4))], cross_y.at[k], cy_s.at[k], cy_r.at[k], device_id=y_peer(k))
+
+    def cross_z_copy(k):
+        return remote(cross_z.at[0], cross_z.at[k], cz_s.at[k], cz_r.at[k], device_id=z_peer(k))
+
+    def cross_part_copy(k):
+        spot = cross_part.at[eight(y)]
+        return remote(spot, spot, cp_s.at[k], cp_r.at[k], device_id=y_peer(k))
+
+    def cross_share_copy(k):
+        spot = cross_sum.at[rows_of(row)]
+        return remote(spot, spot, cg_s.at[k], cg_r.at[k], device_id=row_peer(k))
+
+    def window_copy(k):
+        return remote(window, window_in.at[k], win_s.at[k], win_r.at[k], device_id=row_peer(k))
+
+    def band_copy(k):
+        return remote(band, bands.at[col], bd_s.at[k], bd_r.at[k], device_id=col_peer(k))
+
+    send_rows(0)
+    one_hi, one_lo = split(panel_one[...])
+    two_hi, two_lo = split(panel_two[...])
+    cross[...] = dot3(two_hi.T, two_lo.T, one_hi, one_lo)
+    v_hi[:, :CAP], v_hi[:, CAP:] = two_hi, one_hi
+    v_lo[:, :CAP], v_lo[:, CAP:] = two_lo, one_lo
+    each(1, 8, lambda k: cross_copy(k).start())
+    gram_high[...] = jnp.zeros_like(gram_high)
+    gram_low[...] = jnp.zeros_like(gram_low)
+    each(1, 8, lambda k: cross_copy(k).wait())
+    piece = cross[rows_of(row)]
+    for k in range(1, 8):
+        piece = piece + cross_in[k]
+    cross_mine[...] = piece
+    each(1, 4, lambda k: cross_y_copy(k).start())
+    each(1, 3, send_rows)
+    each(3, 8, lambda j: load(j).wait())
     own = pltpu.make_async_copy(held.at[:, pl.ds(pl.multiple_of(col * width, 128), width)], spread.at[col], own_sem)
     own.start()
-
-    gram_high[...] = jnp.zeros_like(gram_high)
-    gram_low[...] = jnp.zeros_like(gram_low)
-    rhs_t = (((1,), (1,)), ((), ()))
 
     def gram_step(s):
         hi, lo = split(held[:, pl.ds(pl.multiple_of(s * 1024, 1024), 1024)])
@@ -352,73 +422,61 @@
         shift = 1 << bit
         offsets = jnp.maximum(offsets, jnp.where(lanes >= shift, pltpu.roll(offsets, shift, 1), 0))
     offset = offsets[:1]
-    own_start, own_count = jnp.int32(0), jnp.int32(0)
+    own_count = jnp.int32(0)
     for t in range(16):
-        own_start = own_start + jnp.where(t < col, counts[t], 0)
         own_count = own_count + jnp.where(t == col, counts[t], 0)
     live = lane < own_count
     low = gram_low[...]
     window[...] = cluster_window(gram_high[...] + (low + low.T), offset)
-    one_hi, one_lo = split(panel_one[...])
-    two_hi, two_lo = split(panel_two[...])
-    turned_hi, turned_lo = two_hi.T, two_lo.T
-    cross[...] = dot3(turned_hi, turned_lo, one_hi, one_lo)
-    v_hi[:, :CAP], v_hi[:, CAP:] = two_hi, one_hi
-    v_lo[:, :CAP], v_lo[:, CAP:] = two_lo, one_lo
-
-    def window_copy(k):
-        return remote(window, window_in.at[k], win_s.at[k], win_r.at[k], device_id=row_peer(k))
-
-    def cross_copy(k):
-        return remote(cross.at[rows_of(lax.rem(row + k, 8))], cross_in.at[k], cr_s.at[k], cr_r.at[k], device_id=row_peer(k))
-
     each(1, 8, lambda k: window_copy(k).start())
-    each(1, 8, lambda k: cross_copy(k).start())
+    each(1, 4, lambda k: cross_y_copy(k).wait())
+    piece = cross_mine[eight(y)]
+    for k in range(1, 4):
+        piece = piece + cross_y[k]
+    cross_z[0] = piece
+    each(1, 4, lambda k: cross_z_copy(k).start())
+    each(3, 4, lambda j: each(1, 16, lambda k: move(j, k).start()))
     each(1, 8, lambda k: window_copy(k).wait())
-    each(1, 8, lambda k: cross_copy(k).wait())
-    piece = cross[rows_of(row)]
-    for k in range(1, 8):
-        piece = piece + cross_in[k]
-    cross_mine[...] = piece
     window_in[0] = window[...]
     total = window_in[row]
     for r in range(1, 8):
         total = total + window_in[lax.rem(row + 8 - r, 8)]
-    band[:CM] = inverse_band(total, offset, live)
-    band[CM:CM + 1] = offset.astype(jnp.float32)
-    band[CM + 1:CM + 2] = jnp.broadcast_to(lax.rem(own_start, 8), (1, CAP)).astype(jnp.float32)
-    band[CM + 2:] = jnp.zeros((6, CAP), jnp.float32)
-
-    def band_copy(k):
-        return remote(band, bands.at[col], bd_s.at[k], bd_r.at[k], device_id=col_peer(k))
-
-    def cross_all_copy(k):
-        return remote(cross_mine, cross_all.at[k], ca_s.at[k], ca_r.at[k], device_id=col_peer(k))
-
-    def cross_share_copy(k):
-        spot = cross_sum.at[rows_of(row)]
-        return remote(spot, spot, cg_s.at[k], cg_r.at[k], device_id=row_peer(k))
-
-    each(1, 16, lambda k: cross_all_copy(k).start())
+    band[...] = inverse_band(total, offset, live)
     each(1, 16, lambda k: band_copy(k).start())
-    for j in range(EARLY, 8):
-        each(1, 16, lambda k: move(j, k).start())
     bands[col] = band[...]
+    each(1, 4, lambda k: cross_z_copy(k).wait())
+    piece = cross_z[0]
+    for k in range(1, 4):
+        piece = piece + cross_z[k]
+    cross_part[eight(y)] = piece
+    each(1, 4, lambda k: cross_part_copy(k).start())
+    each(4, 8, lambda j: each(1, 16, lambda k: move(j, k).start()))
     f_hi, f_lo = split(factor_one[...].T)
     one = contract(f_hi, one_hi, rhs_t) + (contract(f_hi, one_lo, rhs_t) + contract(f_lo, one_hi, rhs_t))
     hi, lo = split(one)
     b_hi[CAP:], b_lo[CAP:] = hi, lo
-    each(1, 16, lambda k: cross_all_copy(k).wait())
-    piece = cross_mine[...]
-    for k in range(1, 16):
-        piece = piece + cross_all[k]
-    cross_sum[rows_of(row)] = piece
+    each(1, 4, lambda k: cross_part_copy(k).wait())
+    cross_sum[rows_of(row)] = cross_part[...]
     each(1, 8, lambda k: cross_share_copy(k).start())
     each(1, 16, lambda k: band_copy(k).wait())
+    depth = lax.broadcasted_iota(jnp.int32, (CM, CAP), 0)
+
+    def wide_copies(s):
+        return (
+            pltpu.make_async_copy(wide_hi.at[s], t_hi.at[s], wide_sem.at[s, 0]),
+            pltpu.make_async_copy(wide_lo.at[s], t_lo.at[s], wide_sem.at[s, 1]),
+        )
 
     def widen(s):
-        hi, lo = split(dense_rows(bands[s, :CM], bands[s, CM:CM + 1].astype(jnp.int32), bands[s, CM + 1:CM + 2].astype(jnp.int32)))
-        t_hi[s], t_lo[s] = hi, lo
+        start = jnp.int32(0)
+        for t in range(16):
+            start = start + jnp.where(t < s, counts[t], 0)
+        rows = bands[s]
+        last = jnp.max(jnp.where(rows != 0.0, depth, 0), axis=0, keepdims=True)
+        hi, lo = split(dense_rows(rows, lane - last, jnp.broadcast_to(lax.rem(start, 8), (1, CAP))))
+        wide_hi[s], wide_lo[s] = hi, lo
+        for copy in wide_copies(s):
+            copy.start()
 
     each(0, 16, widen)
     each(1, 8, lambda k: cross_share_copy(k).wait())
@@ -428,6 +486,12 @@
     hi, lo = split(dot3(f_hi, f_lo, rest_hi, rest_lo))
     b_hi[:CAP], b_lo[:CAP] = hi, lo
     own.wait()
+
+    def finish_wide(s):
+        for copy in wide_copies(s):
+            copy.wait()
+
+    each(0, 16, finish_wide)
 
     def finish(j):
         each(1, 16, lambda k: move(j, k).wait())
@@ -449,37 +513,40 @@
             half(16, TALL, CAP), half(16, TALL, CAP), half(width, 512), half(width, 512), half(512, width), half(512, width),
         ),
         in_specs=[pl.BlockSpec(memory_space=pltpu.SMEM), hbm, vmem, vmem, vmem, vmem, vmem],
-        out_specs=(hbm, vmem, vmem, vmem, vmem, vmem, vmem),
+        out_specs=(hbm, hbm, hbm, vmem, vmem, vmem, vmem),
         scratch_shapes=[
             V(raw.shape, jnp.float32), tile(CAP), tile(CAP), tile(CAP), tile(CM), tile(8, CM), tile(8, ROWS), tile(ROWS),
-            tile(16, ROWS), tile(CAP), tile(40), tile(16, 40),
-            D((8,)), D, D((8, 16)), D((8, 16)), D((8,)), D((8,)), D((8,)), D((8,)), D((16,)), D((16,)), D((8,)), D((8,)),
-            D((16,)), D((16,)),
+            tile(4, 8), tile(4, 8), tile(ROWS), tile(CAP), tile(CM), tile(16, CM),
+            V((16, TALL, CAP), jnp.bfloat16), V((16, TALL, CAP), jnp.bfloat16),
+            D((8,)), D, D((8, 16)), D((8, 16)), D((8,)), D((8,)), D((8,)), D((8,)), D((4,)), D((4,)), D((4,)), D((4,)),
+            D((4,)), D((4,)), D((8,)), D((8,)), D((16,)), D((16,)), D((16, 2)),
         ],
         compiler_params=pltpu.CompilerParams(collective_id=3, has_side_effects=True, vmem_limit_bytes=56 * 1024 * 1024),
     )(counts, raw, labels, panel_one, factor_one, panel_two, factor_two)
 
 
 def order_kernel(start_ref, t_hi, t_lo, raw_ref, held):
-    start = start_ref[pl.program_id(0)]
-    lead = lax.rem(start, 8)
-    base = pl.multiple_of(start - lead, 8)
-    z_hi, z_lo = split(raw_ref[0])
-    rows = dot3(t_hi[0], t_lo[0], z_hi, z_lo)
-    kept = lax.broadcasted_iota(jnp.int32, (8, rows.shape[1]), 0) < lead
-    held[pl.ds(base, 8), :] = jnp.where(kept, held[pl.ds(base, 8), :], rows[:8])
-    held[pl.ds(base + 8, CAP), :] = rows[8:CAP + 8]
+    for i in range(raw_ref.shape[0]):
+        start = start_ref[pl.program_id(0) * raw_ref.shape[0] + i]
+        lead = lax.rem(start, 8)
+        base = pl.multiple_of(start - lead, 8)
+        z_hi, z_lo = split(raw_ref[i])
+        rows = dot3(t_hi[i], t_lo[i], z_hi, z_lo)
+        kept = lax.broadcasted_iota(jnp.int32, (8, rows.shape[1]), 0) < lead
+        held[pl.ds(base, 8), :] = jnp.where(kept, held[pl.ds(base, 8), :], rows[:8])
+        held[pl.ds(base + 8, CAP), :] = rows[8:CAP + 8]
 
 
 def order_rows(starts, t_hi, t_lo, spread):
     width = spread.shape[2]
-    factor = pl.BlockSpec((1, TALL, CAP), lambda s, starts: (s, 0, 0))
+    group = 2
+    factor = pl.BlockSpec((group, TALL, CAP), lambda s, starts: (s, 0, 0))
     return pl.pallas_call(
         order_kernel,
         grid_spec=pltpu.PrefetchScalarGridSpec(
             num_scalar_prefetch=1,
-            grid=(16,),
-            in_specs=[factor, factor, pl.BlockSpec((1, CAP, width), lambda s, starts: (s, 0, 0))],
+            grid=(16 // group,),
+            in_specs=[factor, factor, pl.BlockSpec((group, CAP, width), lambda s, starts: (s, 0, 0))],
             out_specs=pl.BlockSpec((2048 + CAP + 8, width), lambda s, starts: (0, 0)),
         ),
         out_shape=jax.ShapeDtypeStruct((2048 + CAP + 8, width), jnp.float32),

time: 288 us -> 274 us (0.951)
  Pallas kernels: 280 us -> 266 us
    pallas_call x1, Pallas kernels: 145 us -> 138 us  [front(): pl.pallas_call(front_kernel, out_shape=(jax.ShapeDtypeStruct((16, CAP, wi...]
    pallas_call x1, Pallas kernels: 17.7 us -> 13.8 us  [order_rows(): pl.pallas_call(order_kernel, grid_spec=pltpu.PrefetchScalarGridSpec(num_s...]
    pallas_call x1, Pallas kernels: 118 us -> 115 us  [back_transform(): pl.pallas_call(back_transform_kernel, out_shape=jax.ShapeDtypeStruct((128...]
where the time goes in v4:
time: 274 us
  Pallas kernels  266 us (97%)
  local copies, waits for them, and re-layouts  6.08 us (2%)
    pallas_call x1, Pallas kernels, front(): pl.pallas_call(front_kernel, out_shape=(jax.ShapeDtypeStruct((16, CAP, wi...  138 us
    pallas_call x1, Pallas kernels, back_transform(): pl.pallas_call(back_transform_kernel, out_shape=jax.ShapeDtypeStruct((128...  115 us
    pallas_call x1, Pallas kernels, order_rows(): pl.pallas_call(order_kernel, grid_spec=pltpu.PrefetchScalarGridSpec(num_s...  13.8 us

profile of v4, /device:TPU:0, one launch (start us, length us, event | category | flops | bytes accessed | tf_op | source)
XLA Modules:
  0.0 273.8 jit_solution(16945531285775720116)
XLA Ops:
  0.0 0.7 copy.9
  0.8 0.1 reduce
  0.9 1.2 sub.3.start_ref
  2.1 137.9 %shard_map.73 = (f32[16,256,640]{2,1,0:T(8,128)}, bf16[16,272,256]{2,1,0:T(8,128)(2,1)}, bf16[16,272,256]{2,1,0:T(8,128)(2,1)}, bf16[640,512]{1,0:T(8,128)(2,1)}...) custom-call(s32[16]{0:T(128)} %counts.1, f32[256,10240]{1,0:T(8,128)} %raw.1, ...), custom_call_target="tpu_custom_call" | custom-call | tf_op jit(solution)/shard_map/pallas_call | solution.py:509
  140.0 13.8 %shard_map.74.rows_in = f32[2312,640]{1,0:T(8,128)} custom-call(s32[16]{0:T(128)} %sub.3.start_ref, bf16[16,272,256]{2,1,0:T(8,128)(2,1)} %get-tuple-element.12.t_hi, bf16[16,272,256]{2,1,0:T(8,128)(2,1)} %get-tuple-element.13.t_lo, f32[16,256,640]{2,1,0:T(8,128)} %get-tuple-element.14.raw_ref), custom_call_target="tpu_custom_call" | custom-call | tf_op jit(solution)/shard_map/pallas_call | solution.py:544
  153.8 114.7 %shard_map.75 = f32[128,10240]{1,0:T(8,128)} custom-call(f32[2312,640]{1,0:T(8,128)} %shard_map.74.rows_in, bf16[640,512]{1,0:T(8,128)(2,1)} %get-tuple-element.15.v_hi_in, bf16[640,512]{1,0:T(8,128)(2,1)} %get-tuple-element.16.v_lo_in, bf16[512,640]{1,0:T(8,128)(2,1)} %get-tuple-element.17.b_hi_in, bf16[512,640]{1,0:T(8,128)(2,1)} %get-tuple-element.18.b_lo_in), custom_call_target="tpu_custom_call" | custom-call | tf_op jit(solution)/shard_map/pallas_call | solution.py:238
  268.5 5.3 %copy.11 = f32[128,10240]{1,0:T(8,128)} copy(f32[128,10240]{1,0:T(8,128)} %shard_map.75) | data formatting | bytes 10485760
  (1 shorter events, 0.0 us)

commit v5 on v4

--- a/solution.py
+++ b/solution.py
@@ -121,7 +121,7 @@
         return remote(spot, spot, gc_s.at[c], gc_r.at[c], device_id=partner)
 
     def window(c, source):
-        return out.at[pl.ds(pl.multiple_of(c * 16, 16), 16), pl.ds(pl.multiple_of(source * width, 128), width)]
+        return out.at[source, pl.ds(pl.multiple_of(c * 16, 16), 16)]
 
     def slab(c, target):
         return result.at[c, pl.ds(pl.multiple_of(target * 16, 16), 16)]
@@ -202,8 +202,8 @@
         own_copy(c).start()
 
     stages = (
-        (1, fold_core), (2, fold_a), (3, fold_b), (5, fold_plane), (7, gather_plane), (8, forward), (9, share),
-        (10, correct), (0, project),
+        (8, correct), (7, share), (6, forward), (5, gather_plane), (4, fold_plane), (3, fold_b), (2, fold_a),
+        (1, fold_core), (0, project),
     )
 
     def tick(t, carry):
@@ -219,7 +219,7 @@
     lax.fori_loop(0, 8, tick, 0)
     panels[2].wait()
     panels[3].wait()
-    lax.fori_loop(8, CHUNKS + 10, tick, 0)
+    lax.fori_loop(8, CHUNKS + 8, tick, 0)
 
     def finish(c):
         each(1, 16, lambda k: move_copy(c, k).wait())
@@ -237,7 +237,7 @@
     tile = lambda *lead: V((*lead, 8, 128), jnp.float32)
     return pl.pallas_call(
         back_transform_kernel,
-        out_shape=jax.ShapeDtypeStruct((128, 16 * width), jnp.float32),
+        out_shape=jax.ShapeDtypeStruct((16, 16 * CHUNKS, width), jnp.float32),
         in_specs=[pl.BlockSpec(memory_space=pl.ANY)] * 5,
         out_specs=pl.BlockSpec(memory_space=pl.ANY),
         scratch_shapes=[
@@ -525,9 +525,11 @@
     )(counts, raw, labels, panel_one, factor_one, panel_two, factor_two)
 
 
-def order_kernel(start_ref, t_hi, t_lo, raw_ref, held):
+def order_kernel(counts, t_hi, t_lo, raw_ref, held):
     for i in range(raw_ref.shape[0]):
-        start = start_ref[pl.program_id(0) * raw_ref.shape[0] + i]
+        start = jnp.int32(0)
+        for t in range(16):
+            start = start + jnp.where(t < pl.program_id(0) * raw_ref.shape[0] + i, counts[t], 0)
         lead = lax.rem(start, 8)
         base = pl.multiple_of(start - lead, 8)
         z_hi, z_lo = split(raw_ref[i])
@@ -537,29 +539,56 @@
         held[pl.ds(base + 8, CAP), :] = rows[8:CAP + 8]
 
 
-def order_rows(starts, t_hi, t_lo, spread):
+def order_rows(counts, t_hi, t_lo, spread):
     width = spread.shape[2]
-    group = 2
-    factor = pl.BlockSpec((group, TALL, CAP), lambda s, starts: (s, 0, 0))
+    group = 4
+    factor = pl.BlockSpec((group, TALL, CAP), lambda s, counts: (s, 0, 0))
     return pl.pallas_call(
         order_kernel,
         grid_spec=pltpu.PrefetchScalarGridSpec(
             num_scalar_prefetch=1,
             grid=(16 // group,),
-            in_specs=[factor, factor, pl.BlockSpec((group, CAP, width), lambda s, starts: (s, 0, 0))],
-            out_specs=pl.BlockSpec((2048 + CAP + 8, width), lambda s, starts: (0, 0)),
+            in_specs=[factor, factor, pl.BlockSpec((group, CAP, width), lambda s, counts: (s, 0, 0))],
+            out_specs=pl.BlockSpec((2048 + CAP + 8, width), lambda s, counts: (0, 0)),
         ),
         out_shape=jax.ShapeDtypeStruct((2048 + CAP + 8, width), jnp.float32),
-    )(starts, t_hi, t_lo, spread)
+    )(counts, t_hi, t_lo, spread)
+
+
+def by_row_kernel(blocks, out, held, in_sem, out_sem):
+    count, _, width = blocks.shape
+    loads = [pltpu.make_async_copy(blocks.at[t], held.at[t], in_sem.at[t]) for t in range(count)]
+    stores = [
+        pltpu.make_async_copy(held.at[t], out.at[:, pl.ds(t * width, width)], out_sem.at[t]) for t in range(count)
+    ]
+    for load in loads:
+        load.start()
+    for load, store in zip(loads, stores):
+        load.wait()
+        store.start()
+    for store in stores:
+        store.wait()
+
+
+def by_row(blocks):
+    count, rows, width = blocks.shape
+    return pl.pallas_call(
+        by_row_kernel,
+        out_shape=jax.ShapeDtypeStruct((rows, count * width), jnp.float32),
+        in_specs=[pl.BlockSpec(memory_space=pl.ANY)],
+        out_specs=pl.BlockSpec(memory_space=pl.ANY),
+        scratch_shapes=[
+            pltpu.VMEM(blocks.shape, jnp.float32), pltpu.SemaphoreType.DMA((count,)), pltpu.SemaphoreType.DMA((count,))
+        ],
+    )(blocks)
 
 
 def body(raw_vectors, interval_count, cluster_of, panel_one, factor_one, panel_two, factor_two):
     spread, t_hi, t_lo, v_hi, v_lo, b_hi, b_lo = front(
         interval_count, raw_vectors, cluster_of, panel_one, factor_one, panel_two, factor_two
     )
-    starts = jnp.cumsum(interval_count) - interval_count
-    ordered = order_rows(starts, t_hi, t_lo, spread)
-    return back_transform(ordered, v_hi, v_lo, b_hi, b_lo)
+    ordered = order_rows(interval_count, t_hi, t_lo, spread)
+    return by_row(back_transform(ordered, v_hi, v_lo, b_hi, b_lo))
 
 
 def solution(mesh):

time: 274 us -> 267 us (0.974)
  local copies, waits for them, and re-layouts: 6.08 us -> 0 us
    unnamed x1 -> x0, local copies, waits for them, and re-layouts: 5.35 us -> none
    pallas_call x1 -> x2, Pallas kernels: 115 us -> 117 us  [the longest x1 112 us: back_transform(): pl.pallas_call(back_transform_kernel, out_shape=jax.ShapeDtypeStruct((16,...]
where the time goes in v5:
time: 267 us
  Pallas kernels  267 us (100%)
    pallas_call x1, Pallas kernels, front(): pl.pallas_call(front_kernel, out_shape=(jax.ShapeDtypeStruct((16, CAP, wi...  138 us
    pallas_call x1, Pallas kernels, back_transform(): pl.pallas_call(back_transform_kernel, out_shape=jax.ShapeDtypeStruct((16,...  112 us
    pallas_call x1, Pallas kernels, order_rows(): pl.pallas_call(order_kernel, grid_spec=pltpu.PrefetchScalarGridSpec(num_s...  12.3 us

profile of v5, /device:TPU:0, one launch (start us, length us, event | category | flops | bytes accessed | tf_op | source)
XLA Modules:
  0.0 266.8 jit_solution(6539712488863010684)
XLA Ops:
  0.0 137.9 %shard_map.73 = (f32[16,256,640]{2,1,0:T(8,128)}, bf16[16,272,256]{2,1,0:T(8,128)(2,1)}, bf16[16,272,256]{2,1,0:T(8,128)(2,1)}, bf16[640,512]{1,0:T(8,128)(2,1)}...) custom-call(s32[16]{0:T(128)} %counts.3, f32[256,10240]{1,0:T(8,128)} %raw.1, ...), custom_call_target="tpu_custom_call" | custom-call | tf_op jit(solution)/shard_map/pallas_call | solution.py:509
  137.9 12.3 %shard_map.74.rows_in = f32[2312,640]{1,0:T(8,128)} custom-call(s32[16]{0:T(128)} %counts.3, bf16[16,272,256]{2,1,0:T(8,128)(2,1)} %get-tuple-element.12.t_hi, bf16[16,272,256]{2,1,0:T(8,128)(2,1)} %get-tuple-element.13.t_lo, f32[16,256,640]{2,1,0:T(8,128)} %get-tuple-element.14.raw_ref), custom_call_target="tpu_custom_call" | custom-call | tf_op jit(solution)/shard_map/pallas_call | solution.py:546
  150.3 111.6 %shard_map.75.blocks = f32[16,128,640]{2,1,0:T(8,128)} custom-call(f32[2312,640]{1,0:T(8,128)} %shard_map.74.rows_in, bf16[640,512]{1,0:T(8,128)(2,1)} %get-tuple-element.15.v_hi_in, bf16[640,512]{1,0:T(8,128)(2,1)} %get-tuple-element.16.v_lo_in, bf16[512,640]{1,0:T(8,128)(2,1)} %get-tuple-element.17.b_hi_in, bf16[512,640]{1,0:T(8,128)(2,1)} %get-tuple-element.18.b_lo_in), custom_call_target="tpu_custom_call" | custom-call | tf_op jit(solution)/shard_map/pallas_call | solution.py:238
  261.9 4.9 %shard_map.76 = f32[128,10240]{1,0:T(8,128)} custom-call(f32[16,128,640]{2,1,0:T(8,128)} %shard_map.75.blocks), custom_call_target="tpu_custom_call" | custom-call | tf_op jit(solution)/shard_map/pallas_call | solution.py:575
